TPU v7x, 512 devices: a whole 4x8x8 slice. The times are simulated.
512 devices in a mesh: chain: 2 (over x_lo), slab: 128 (over x_hi, z, y), vis: 2 (over core).
Axes of the slice: x: 4 (x_hi: 2, x_lo: 2; x = x_hi * 2 + x_lo), y: 8, z: 8, core: 2. Of those that a mesh axis runs over, the one named last changes fastest.
Arguments:
- screens: float32 [4, 2048, 2048], P(('chain', 'vis'), 'slab'), parts along dimension 0, may hold values from -6 to 6
- image: float32 [4096, 2048], P(('chain', 'slab')), parts along dimension 0, may hold values from -6 to 6
- vis_row: int32 [32768], P('slab'), may hold values from 0 to 2047
- vis_block: int32 [32768, 1], P('slab'), may hold values from 0 to 127; in each aligned block of 256 rows (0 to 255, 256 to 511, ...) at most 6 rows name the same one
- vis_column: int32 [32768], P('slab'), may hold values from 0 to 7
- vis_real: float32 [32768], P('slab'), may hold values from -6 to 6
- vis_imag: float32 [32768], P('slab'), may hold values from -6 to 6
- vis_weight: float32 [32768], P('slab'), may hold values from 0.5 to 4
Outputs:
- screen_grad: float32 [4, 2048, 2048], P(('chain', 'vis'), 'slab'), parts along dimension 0
There are 2 independent parts, one for each index of `chain`. A program takes and returns all parts, laid end to end along the dimension named above; an argument that names none is the same for every part. Nothing has to cross between parts.
Inputs may be any that keep to these rules, and one draw needn't show every extreme that they name: `vis_block`: among the 256 visibilities of one index of slab, at most 6 name any one block; in every draw some block of some index holds exactly 6.
All inputs are finite; a program needn't handle non-finite values.
Results may differ from a plain program's by a relative error of at most 0.013.
Values may be sent and summed in bfloat16 or wider, within the bound.
No kernel may reach another device: no remote copies, remote signals or barrier semaphores. Data moves between devices by JAX's collectives and lax.ppermute only.
A program may use at most 64 MiB of HBM per device.

v0:
```python
import math

import jax
import jax.numpy as jnp
from jax import lax
from jax.sharding import PartitionSpec as P

refract = 1.0
rank_rows = 512
sample_rows = 256
table_rows = 256


def with_halo(cells, sides, width):
    for axis, dim in sides:
        count = lax.axis_size(axis)
        head = lax.slice_in_dim(cells, 0, width, axis=dim)
        tail = lax.slice_in_dim(cells, cells.shape[dim] - width, cells.shape[dim], axis=dim)
        cells = jnp.concatenate(
            [
                lax.ppermute(tail, axis, [(i, (i + 1) % count) for i in range(count)]),
                cells,
                lax.ppermute(head, axis, [((i + 1) % count, i) for i in range(count)]),
            ],
            axis=dim,
        )
    return cells


def twiddle(first, second, length):
    phase = (first[:, None] * second[None, :] % length).astype(jnp.float32) * (
        2.0 * math.pi / length
    )
    return (jnp.cos(phase).astype(jnp.bfloat16), jnp.sin(phase).astype(jnp.bfloat16))


def col_slope(field):
    return (
        8.0 * (jnp.roll(field, -1, -1) - jnp.roll(field, 1, -1))
        - (jnp.roll(field, -2, -1) - jnp.roll(field, 2, -1))
    ) / 12.0


def col_adjoint(field):
    return (
        8.0 * (jnp.roll(field, 1, -1) - jnp.roll(field, -1, -1))
        - (jnp.roll(field, 2, -1) - jnp.roll(field, -2, -1))
    ) / 12.0


def row_slope(padded, row_count):
    return (
        8.0 * (padded[..., 3 : row_count + 3, :] - padded[..., 1 : row_count + 1, :])
        - (padded[..., 4 : row_count + 4, :] - padded[..., 0:row_count, :])
    ) / 12.0


def row_adjoint(padded, row_count):
    return (
        8.0 * (padded[..., 1 : row_count + 1, :] - padded[..., 3 : row_count + 3, :])
        - (padded[..., 0:row_count, :] - padded[..., 4 : row_count + 4, :])
    ) / 12.0


def local(screens, image, vis_row, vis_block, vis_column, vis_real, vis_imag, vis_weight):
    walkers, row_count, grid_size = screens.shape
    slabs = lax.axis_size("slab")
    half_kx = grid_size // 2
    vis_count = vis_row.shape[0]
    capacity = 3 * vis_count // slabs
    unitary = 1.0 / math.sqrt(grid_size)
    positions = jnp.arange(grid_size, dtype=jnp.int32)
    highest = lax.Precision.HIGHEST
    stacked = jnp.concatenate([screens, image[None]], axis=0)
    padded = with_halo(stacked.astype(jnp.bfloat16), (("slab", 1),), 2).astype(stacked.dtype)
    slope_x = col_slope(stacked)
    slope_y = row_slope(padded, row_count)
    joined = image[None] + refract * (
        slope_x[:walkers] * slope_x[walkers][None] + slope_y[:walkers] * slope_y[walkers][None]
    )
    joined_bf = joined.astype(jnp.bfloat16)
    owner_slab = vis_block[:, 0]
    owned = half_kx // slabs
    step_kx = min(table_rows, half_kx)
    real_parts = []
    imag_parts = []
    for offset in range(0, half_kx, step_kx):
        cos_rows, sin_rows = twiddle(
            offset + jnp.arange(step_kx, dtype=jnp.int32), positions, grid_size
        )
        with_cos = jnp.einsum(
            "kc,wrc->wkr", cos_rows, joined_bf, preferred_element_type=jnp.float32
        )
        with_sin = jnp.einsum(
            "kc,wrc->wkr", sin_rows, joined_bf, preferred_element_type=jnp.float32
        )
        real_parts.append((unitary * with_cos).astype(jnp.bfloat16))
        imag_parts.append((-unitary * with_sin).astype(jnp.bfloat16))
    spectra = jnp.stack([jnp.concatenate(real_parts, 1), jnp.concatenate(imag_parts, 1)])
    columns = lax.all_to_all(spectra, "slab", split_axis=2, concat_axis=3, tiled=True)
    payload = jnp.stack(
        [(vis_column * grid_size + vis_row).astype(jnp.float32), vis_real, vis_imag, vis_weight]
    )
    rank_size = math.gcd(rank_rows, vis_count)
    lower = (jnp.arange(rank_size)[:, None] > jnp.arange(rank_size)[None, :]).astype(jnp.float32)
    owner_hot = (owner_slab[:, None] == jnp.arange(slabs, dtype=jnp.int32)[None, :]).astype(
        jnp.float32
    )

    def rank_step(seen, hot_rows):
        before = jnp.dot(lower, hot_rows, precision=highest) + seen[None, :]
        return (seen + jnp.sum(hot_rows, 0), jnp.sum(before * hot_rows, 1))

    _, ranks = lax.scan(
        rank_step,
        jnp.zeros((slabs,), jnp.float32),
        owner_hot.reshape(vis_count // rank_size, rank_size, slabs),
    )
    destination = owner_slab * capacity + ranks.reshape(vis_count).astype(jnp.int32)
    buckets = (
        jnp.zeros((4, slabs * capacity), jnp.float32)
        .at[:, destination]
        .set(payload)
        .reshape(4, slabs, capacity)
    )
    arrived = lax.all_to_all(buckets, "slab", split_axis=1, concat_axis=1, tiled=True).reshape(
        4, slabs * capacity
    )
    span = walkers * owned
    flat = columns.reshape(2 * span, grid_size)
    total_slots = slabs * capacity
    step_rows = math.gcd(sample_rows, total_slots)
    owned_ids = jnp.arange(owned, dtype=jnp.int32)
    zeros_grid = jnp.zeros((span, grid_size), jnp.float32)

    def sample_step(index, sums):
        block_data = lax.dynamic_slice_in_dim(arrived, index * step_rows, step_rows, 1)
        cell_code = block_data[0].astype(jnp.int32)
        row_freq = cell_code % grid_size
        col_freq = cell_code // grid_size
        cos_rows, sin_rows = twiddle(row_freq, positions, grid_size)
        with_cos = lax.dot_general(
            cos_rows, flat, (((1,), (1,)), ((), ())), preferred_element_type=jnp.float32
        ).reshape(step_rows, 2, walkers, owned)
        with_sin = lax.dot_general(
            sin_rows, flat, (((1,), (1,)), ((), ())), preferred_element_type=jnp.float32
        ).reshape(step_rows, 2, walkers, owned)
        chooser = (col_freq[:, None] == owned_ids[None, :]).astype(jnp.float32)
        model_real = unitary * jnp.sum((with_cos[:, 0] + with_sin[:, 1]) * chooser[:, None, :], -1)
        model_imag = unitary * jnp.sum((with_cos[:, 1] - with_sin[:, 0]) * chooser[:, None, :], -1)
        error_real = (block_data[3][:, None] * (model_real - block_data[1][:, None])).astype(
            jnp.bfloat16
        )
        error_imag = (block_data[3][:, None] * (model_imag - block_data[2][:, None])).astype(
            jnp.bfloat16
        )
        spread = jnp.concatenate(
            [
                (error_real[:, :, None] * chooser[:, None, :]).reshape(step_rows, span),
                (error_imag[:, :, None] * chooser[:, None, :]).reshape(step_rows, span),
            ],
            1,
        ).astype(jnp.bfloat16)
        back_cos = lax.dot_general(
            spread, cos_rows, (((0,), (0,)), ((), ())), preferred_element_type=jnp.float32
        )
        back_sin = lax.dot_general(
            spread, sin_rows, (((0,), (0,)), ((), ())), preferred_element_type=jnp.float32
        )
        return (
            sums[0] + back_cos[:span] - back_sin[span:],
            sums[1] + back_sin[:span] + back_cos[span:],
        )

    sum_real, sum_imag = lax.fori_loop(
        0, total_slots // step_rows, sample_step, (zeros_grid, zeros_grid)
    )
    adjoint = (
        (unitary * jnp.stack([sum_real, sum_imag]))
        .astype(jnp.bfloat16)
        .reshape(2, walkers, owned, grid_size)
    )
    returned = lax.all_to_all(adjoint, "slab", split_axis=3, concat_axis=2, tiled=True)
    gradient = jnp.zeros((walkers, row_count, grid_size), jnp.float32)
    for offset in range(0, half_kx, step_kx):
        cos_rows, sin_rows = twiddle(
            offset + jnp.arange(step_kx, dtype=jnp.int32), positions, grid_size
        )
        part_real = returned[0][:, offset : offset + step_kx, :]
        part_imag = returned[1][:, offset : offset + step_kx, :]
        gradient = gradient + jnp.einsum(
            "wkr,kc->wrc", part_real, cos_rows, preferred_element_type=jnp.float32
        )
        gradient = gradient - jnp.einsum(
            "wkr,kc->wrc", part_imag, sin_rows, preferred_element_type=jnp.float32
        )
    gradient = unitary * gradient
    push_x = refract * slope_x[walkers][None] * gradient
    push_y = refract * slope_y[walkers][None] * gradient
    padded_y = with_halo(push_y.astype(jnp.bfloat16), (("slab", 1),), 2).astype(push_y.dtype)
    return col_adjoint(push_x) + row_adjoint(padded_y, row_count)


def solution(mesh):
    in_specs = (
        P(("chain", "vis"), "slab", None),
        P(("chain", "slab"), None),
        P("slab"),
        P("slab", None),
        P("slab"),
        P("slab"),
        P("slab"),
        P("slab"),
    )
    out_specs = P(("chain", "vis"), "slab", None)
    return jax.shard_map(local, mesh=mesh, in_specs=in_specs, out_specs=out_specs, check_vma=False)
```

profile of v0, /device:TPU:2, one launch (start us, length us, event | category | flops | bytes accessed | tf_op | source)
XLA Modules:
  0.0 358.0 jit_solution(11313475501157636354)
XLA Ops:
  4.5 13.8 %collective-permute-start.1 = (bf16[2,2,2048]{2,1,0:T(2,128)(2,1)S(1)}, bf16[2,2,2048]{2,1,0:T(2,128)(2,1)S(1)}, u32[]{:S(2)}, u32[]{:S(2)}) collective-permute-start(bf16[2,2,2048]{2,1,0:T(2,128)(2,1)S(1)} %get-tuple-element.290), channel_id=1, source_target_pairs={{2,0},{4,2},{6,4},{8,6},{10,8},{12,10},{14,12},{16,14},{18,16},{20... | collective-permute-start | bytes 49160 | tf_op jit(solution)/shard_map/ppermute | solution.py:23
  24.2 9.4 %all-to-all-start = ((f32[4,128,6]{2,0,1:T(4,128)}), f32[4,128,6]{2,0,1:T(4,128)S(1)}, u32[]{:S(2)}, u32[]{:S(2)}) async-start(f32[4,128,6]{2,0,1:T(4,128)} %copy.53), calls=%async_computation | async-start | bytes 524288 | tf_op jit(solution)/shard_map/all_to_all | solution.py:126
  34.5 8.8 %fusion.82 = bf16[1,256,16]{1,2,0:T(8,128)(2,1)S(1)} fusion(bf16[16,2048]{1,0:T(8,128)(2,1)S(1)} %fusion.111), kind=kOutput, calls=%fused_computation.142 | convolution fusion | flops 24649728 | bytes 73728 | tf_op jit(solution)/shard_map/kc,wrc->wkr/dot_general | solution.py:94
  43.3 8.1 %fusion.79 = bf16[1,256,16]{1,2,0:T(8,128)(2,1)S(1)} fusion(bf16[16,2048]{1,0:T(8,128)(2,1)S(1)} %fusion.111, s32[256]{0:T(256)S(1)} %iota_add_fusion), kind=kOutput, calls=%fused_computation.139 | convolution fusion | flops 24649728 | bytes 74752 | tf_op jit(solution)/shard_map/kc,wrc->wkr/dot_general | solution.py:94
  51.4 8.0 %fusion.83 = bf16[1,256,16]{1,2,0:T(8,128)(2,1)S(1)} fusion(bf16[16,2048]{1,0:T(8,128)(2,1)S(1)} %fusion.111, s32[256]{0:T(256)S(1)} %iota_add_fusion), kind=kOutput, calls=%fused_computation.143 | convolution fusion | flops 24649728 | bytes 74752 | tf_op jit(solution)/shard_map/kc,wrc->wkr/dot_general | solution.py:91
  59.4 8.6 %fusion.80 = bf16[1,256,16]{1,2,0:T(8,128)(2,1)S(1)} fusion(bf16[16,2048]{1,0:T(8,128)(2,1)S(1)} %fusion.111, s32[256]{0:T(256)S(1)} %iota_add_fusion.1), kind=kOutput, calls=%fused_computation.140 | convolution fusion | flops 24649728 | bytes 74752 | tf_op jit(solution)/shard_map/kc,wrc->wkr/dot_general | solution.py:94
  68.0 8.0 %fusion.84 = bf16[1,256,16]{1,2,0:T(8,128)(2,1)S(1)} fusion(bf16[16,2048]{1,0:T(8,128)(2,1)S(1)} %fusion.111, s32[256]{0:T(256)S(1)} %iota_add_fusion.1), kind=kOutput, calls=%fused_computation.144 | convolution fusion | flops 24649728 | bytes 74752 | tf_op jit(solution)/shard_map/kc,wrc->wkr/dot_general | solution.py:91
  76.0 8.3 %fusion.81 = bf16[1,256,16]{1,2,0:T(8,128)(2,1)S(1)} fusion(bf16[16,2048]{1,0:T(8,128)(2,1)S(1)} %fusion.111, s32[256]{0:T(256)S(1)} %iota_add_fusion.2), kind=kOutput, calls=%fused_computation.141 | convolution fusion | flops 24649728 | bytes 74752 | tf_op jit(solution)/shard_map/kc,wrc->wkr/dot_general | solution.py:94
  84.3 8.0 %fusion.85 = bf16[1,256,16]{1,2,0:T(8,128)(2,1)S(1)} fusion(bf16[16,2048]{1,0:T(8,128)(2,1)S(1)} %fusion.111, s32[256]{0:T(256)S(1)} %iota_add_fusion.2), kind=kOutput, calls=%fused_computation.145 | convolution fusion | flops 24649728 | bytes 74752 | tf_op jit(solution)/shard_map/kc,wrc->wkr/dot_general | solution.py:91
  92.3 8.7 %fusion.86 = bf16[1,256,16]{1,2,0:T(8,128)(2,1)S(1)} fusion(bf16[16,2048]{1,0:T(8,128)(2,1)S(1)} %fusion.111), kind=kOutput, calls=%fused_computation.146 | convolution fusion | flops 24649728 | bytes 73728 | tf_op jit(solution)/shard_map/kc,wrc->wkr/dot_general | solution.py:91
  102.5 16.4 %all-to-all-start.1 = ((bf16[128,2,128]{2,1,0:T(2,128)(2,1)}), bf16[128,2,128]{2,1,0:T(2,128)(2,1)S(1)}, u32[]{:S(2)}, u32[]{:S(2)}) async-start(bf16[128,2,128]{2,1,0:T(2,128)(2,1)} %reshape.696), calls=%async_computation.1 | async-start | bytes 131072 | tf_op jit(solution)/shard_map/all_to_all | solution.py:100
  119.1 14.1 %all-to-all-done.1 = bf16[128,2,128]{2,1,0:T(2,128)(2,1)S(1)} async-done(((bf16[128,2,128]{2,1,0:T(2,128)(2,1)}), bf16[128,2,128]{2,1,0:T(2,128)(2,1)S(1)}, u32[]{:S(2)}, u32[]{:S(2)}) %all-to-all-start.1) | async-done | bytes 65568 | tf_op jit(solution)/shard_map/all_to_all | solution.py:100
  134.6 120.4 %while.24 = (s32[]{:T(128)}, f32[8,2048]{1,0:T(8,128)S(1)}, f32[8,2048]{1,0:T(8,128)S(1)}, f32[4,768]{1,0:T(4,128)S(1)}, bf16[16,2048]{1,0:T(8,128)(2,1)S(1)}, /...) while((s32[]{:T(128)}, f32[8,2048]{1,0:T(8,128)S(1)}, ...), condition=%wide.region_5.6_spmd.clone.clone, body=%wide.region_2.5_spmd.clone.clone.sunk | while | flops 98724360 | bytes 1034473 | solution.py:175
  156.4 7.8 %fusion.213 = f32[256,16]{0,1:T(8,128)S(1)} fusion(bf16[16,2048]{1,0:T(8,128)(2,1)S(1)} %get-tuple-element.382, s32[256]{0:T(256)S(1)} %get-tuple-element.341), kind=kOutput, calls=%fused_computation.16.clone.1 | convolution fusion | flops 24641536 | bytes 82944 | tf_op jit(solution)/shard_map/while/body/eval_jaxpr/dot_general | solution.py:142
  164.3 7.9 %fusion.212 = f32[256,16]{0,1:T(8,128)S(1)} fusion(bf16[16,2048]{1,0:T(8,128)(2,1)S(1)} %get-tuple-element.382, s32[256]{0:T(256)S(1)} %get-tuple-element.341), kind=kOutput, calls=%fused_computation.18.clone.1 | convolution fusion | flops 24641536 | bytes 82944 | tf_op jit(solution)/shard_map/while/body/eval_jaxpr/dot_general | solution.py:145
  172.2 7.9 %fusion.218 = f32[16,2048]{1,0:T(8,128)S(1)} fusion(s32[256]{0:T(256)S(1)} %get-tuple-element.341, bf16[256,8]{0,1:T(8,128)(2,1)S(1)} %get-tuple-element.350, bf16[256,8]{0,1:T(8,128)(2,1)S(1)} %get-tuple-element.351), kind=kOutput, calls=%fused_computation.17.clone.1 | convolution fusion | flops 24657920 | bytes 140288 | tf_op jit(solution)/shard_map/while/body/eval_jaxpr/dot_general | solution.py:167
  180.1 7.8 %fusion.217 = f32[16,2048]{1,0:T(8,128)S(1)} fusion(s32[256]{0:T(256)S(1)} %get-tuple-element.341, bf16[256,8]{0,1:T(8,128)(2,1)S(1)} %get-tuple-element.350, bf16[256,8]{0,1:T(8,128)(2,1)S(1)} %get-tuple-element.351), kind=kOutput, calls=%fused_computation.15.clone.1 | convolution fusion | flops 24657920 | bytes 140288 | tf_op jit(solution)/shard_map/while/body/eval_jaxpr/dot_general | solution.py:164
  188.1 7.8 %fusion.213 = f32[256,16]{0,1:T(8,128)S(1)} fusion(bf16[16,2048]{1,0:T(8,128)(2,1)S(1)} %get-tuple-element.382, s32[256]{0:T(256)S(1)} %get-tuple-element.341), kind=kOutput, calls=%fused_computation.16.clone.1 | convolution fusion | flops 24641536 | bytes 82944 | tf_op jit(solution)/shard_map/while/body/eval_jaxpr/dot_general | solution.py:142
  195.9 7.9 %fusion.212 = f32[256,16]{0,1:T(8,128)S(1)} fusion(bf16[16,2048]{1,0:T(8,128)(2,1)S(1)} %get-tuple-element.382, s32[256]{0:T(256)S(1)} %get-tuple-element.341), kind=kOutput, calls=%fused_computation.18.clone.1 | convolution fusion | flops 24641536 | bytes 82944 | tf_op jit(solution)/shard_map/while/body/eval_jaxpr/dot_general | solution.py:145
  203.9 7.9 %fusion.218 = f32[16,2048]{1,0:T(8,128)S(1)} fusion(s32[256]{0:T(256)S(1)} %get-tuple-element.341, bf16[256,8]{0,1:T(8,128)(2,1)S(1)} %get-tuple-element.350, bf16[256,8]{0,1:T(8,128)(2,1)S(1)} %get-tuple-element.351), kind=kOutput, calls=%fused_computation.17.clone.1 | convolution fusion | flops 24657920 | bytes 140288 | tf_op jit(solution)/shard_map/while/body/eval_jaxpr/dot_general | solution.py:167
  211.8 7.8 %fusion.217 = f32[16,2048]{1,0:T(8,128)S(1)} fusion(s32[256]{0:T(256)S(1)} %get-tuple-element.341, bf16[256,8]{0,1:T(8,128)(2,1)S(1)} %get-tuple-element.350, bf16[256,8]{0,1:T(8,128)(2,1)S(1)} %get-tuple-element.351), kind=kOutput, calls=%fused_computation.15.clone.1 | convolution fusion | flops 24657920 | bytes 140288 | tf_op jit(solution)/shard_map/while/body/eval_jaxpr/dot_general | solution.py:164
  219.8 7.8 %fusion.213 = f32[256,16]{0,1:T(8,128)S(1)} fusion(bf16[16,2048]{1,0:T(8,128)(2,1)S(1)} %get-tuple-element.382, s32[256]{0:T(256)S(1)} %get-tuple-element.341), kind=kOutput, calls=%fused_computation.16.clone.1 | convolution fusion | flops 24641536 | bytes 82944 | tf_op jit(solution)/shard_map/while/body/eval_jaxpr/dot_general | solution.py:142
  227.6 7.9 %fusion.212 = f32[256,16]{0,1:T(8,128)S(1)} fusion(bf16[16,2048]{1,0:T(8,128)(2,1)S(1)} %get-tuple-element.382, s32[256]{0:T(256)S(1)} %get-tuple-element.341), kind=kOutput, calls=%fused_computation.18.clone.1 | convolution fusion | flops 24641536 | bytes 82944 | tf_op jit(solution)/shard_map/while/body/eval_jaxpr/dot_general | solution.py:145
  235.6 7.9 %fusion.218 = f32[16,2048]{1,0:T(8,128)S(1)} fusion(s32[256]{0:T(256)S(1)} %get-tuple-element.341, bf16[256,8]{0,1:T(8,128)(2,1)S(1)} %get-tuple-element.350, bf16[256,8]{0,1:T(8,128)(2,1)S(1)} %get-tuple-element.351), kind=kOutput, calls=%fused_computation.17.clone.1 | convolution fusion | flops 24657920 | bytes 140288 | tf_op jit(solution)/shard_map/while/body/eval_jaxpr/dot_general | solution.py:167
  256.8 19.9 %all_to_all.35 = bf16[128,2,128]{2,1,0:T(2,128)(2,1)S(1)} all-to-all(bf16[128,2,128]{2,1,0:T(2,128)(2,1)S(1)} %reshape.698), channel_id=1, replica_groups=mesh['chain'=2,'slab'=128,'vis'=2] {'slab'}, dimensions={0} | all-to-all | bytes 131072 | tf_op jit(solution)/shard_map/all_to_all | solution.py:183
  287.5 8.2 %convolution_subtract_fusion.3 = f32[16,2048]{1,0:T(8,128)S(1)} fusion(f32[16,2048]{1,0:T(8,128)S(1)} %fusion.87, bf16[1,1024,16]{2,1,0:T(8,128)(2,1)S(1)} %bitcast.172), kind=kOutput, calls=%fused_computation.88 | convolution fusion | flops 24674304 | bytes 327680 | tf_op jit(solution)/shard_map/wkr,kc->wrc/dot_general | solution.py:194
  295.7 8.0 %convolution_add_fusion.2 = f32[16,2048]{1,0:T(8,128)S(1)} fusion(f32[16,2048]{1,0:T(8,128)S(1)} %convolution_subtract_fusion.3, s32[256]{0:T(256)S(1)} %iota_add_fusion.2, bf16[1,1024,16]{2,1,0:T(8,128)(2,1)S(1)} %bitcast.177), kind=kOutput, calls=%fused_computation.87 | convolution fusion | flops 24674304 | bytes 328704 | tf_op jit(solution)/shard_map/wkr,kc->wrc/dot_general | solution.py:191
  303.7 7.9 %convolution_subtract_fusion.2 = f32[16,2048]{1,0:T(8,128)S(1)} fusion(f32[16,2048]{1,0:T(8,128)S(1)} %convolution_add_fusion.2, s32[256]{0:T(256)S(1)} %iota_add_fusion.2, bf16[1,1024,16]{2,1,0:T(8,128)(2,1)S(1)} %bitcast.173), kind=kOutput, calls=%fused_computation.86 | convolution fusion | flops 24674304 | bytes 328704 | tf_op jit(solution)/shard_map/wkr,kc->wrc/dot_general | solution.py:194
  311.6 8.0 %convolution_add_fusion.1 = f32[16,2048]{1,0:T(8,128)S(1)} fusion(f32[16,2048]{1,0:T(8,128)S(1)} %convolution_subtract_fusion.2, s32[256]{0:T(256)S(1)} %iota_add_fusion.1, bf16[1,1024,16]{2,1,0:T(8,128)(2,1)S(1)} %bitcast.178), kind=kOutput, calls=%fused_computation.85 | convolution fusion | flops 24674304 | bytes 328704 | tf_op jit(solution)/shard_map/wkr,kc->wrc/dot_general | solution.py:191
  319.6 8.3 %convolution_subtract_fusion.1 = f32[16,2048]{1,0:T(8,128)S(1)} fusion(f32[16,2048]{1,0:T(8,128)S(1)} %convolution_add_fusion.1, s32[256]{0:T(256)S(1)} %iota_add_fusion.1, bf16[1,1024,16]{2,1,0:T(8,128)(2,1)S(1)} %bitcast.174), kind=kOutput, calls=%fused_computation.84 | convolution fusion | flops 24674304 | bytes 328704 | tf_op jit(solution)/shard_map/wkr,kc->wrc/dot_general | solution.py:194
  335.6 8.1 %slice_multiply_fusion.2 = (f32[1,16,2048]{2,1,0:T(8,128)S(1)}, bf16[1,16,2048]{2,1,0:T(8,128)(2,1)S(1)}) fusion(f32[2,16,2048]{2,1,0:T(8,128)S(1)} %fusion.98, f32[2,16,2048]{2,1,0:T(8,128)S(1)} %fusion.94, f32[16,2048]{1,0:T(8,128)S(1)} %convolution_add_fusion, s32[256]{0:T(256)S(1)} %iota_add_fusion, bf16[1,1024,16]{2,1,0:T(8,128)(2,1)S(1)} %bitcast.175), kind=kOutput, calls=%fused_computation.206 | convolution fusion | flops 24805376 | bytes 656384 | tf_op jit(solution)/shard_map/wkr,kc->wrc/dot_general | solution.py:194
  346.6 9.0 %collective-permute-start.3 = (bf16[1,2,2048]{2,1,0:T(2,128)(2,1)S(1)}, bf16[1,2,2048]{2,1,0:T(2,128)(2,1)S(1)}, u32[]{:S(2)}, u32[]{:S(2)}) collective-permute-start(bf16[1,2,2048]{2,1,0:T(2,128)(2,1)S(1)} %get-tuple-element.292), channel_id=1, source_target_pairs={{2,0},{4,2},{6,4},{8,6},{10,8},{12,10},{14,12},{16,14},{18,16},{20... | collective-permute-start | bytes 24584 | tf_op jit(solution)/shard_map/ppermute | solution.py:23
  (82 shorter events, 47.7 us)
Async XLA Ops:
  1.0 33.2 %collective-permute-start = (bf16[2,2,2048]{2,1,0:T(2,128)(2,1)S(1)}, bf16[2,2,2048]{2,1,0:T(2,128)(2,1)S(1)}, u32[]{:S(2)}, u32[]{:S(2)}) collective-permute-start(bf16[2,2,2048]{2,1,0:T(2,128)(2,1)S(1)} %get-tuple-element.289), channel_id=1, source_target_pairs={{0,2},{2,4},{4,6},{6,8},{8,10},{10,12},{12,14},{14,16},{16,18},{18... | collective-permute-start | bytes 49160 | tf_op jit(solution)/shard_map/ppermute | solution.py:21
  4.5 29.8 %collective-permute-start.1 = (bf16[2,2,2048]{2,1,0:T(2,128)(2,1)S(1)}, bf16[2,2,2048]{2,1,0:T(2,128)(2,1)S(1)}, u32[]{:S(2)}, u32[]{:S(2)}) collective-permute-start(bf16[2,2,2048]{2,1,0:T(2,128)(2,1)S(1)} %get-tuple-element.290), channel_id=1, source_target_pairs={{2,0},{4,2},{6,4},{8,6},{10,8},{12,10},{14,12},{16,14},{18,16},{20... | collective-permute-start | bytes 49160 | tf_op jit(solution)/shard_map/ppermute | solution.py:23
  21.6 11.9 %copy-start = (f32[16,2048]{1,0:T(8,128)S(1)}, f32[16,2048]{1,0:T(8,128)}, u32[]{:S(2)}) copy-start(f32[16,2048]{1,0:T(8,128)} %param.11) | copy-start | bytes 393220
  21.6 11.9 %copy-start.1 = (f32[1,16,2048]{2,1,0:T(8,128)S(1)}, f32[1,16,2048]{2,1,0:T(8,128)}, u32[]{:S(2)}) copy-start(f32[1,16,2048]{2,1,0:T(8,128)} %param.10) | copy-start | bytes 393220
  24.2 78.3 %all-to-all-start = ((f32[4,128,6]{2,0,1:T(4,128)}), f32[4,128,6]{2,0,1:T(4,128)S(1)}, u32[]{:S(2)}, u32[]{:S(2)}) async-start(f32[4,128,6]{2,0,1:T(4,128)} %copy.53), calls=%async_computation | async-start | bytes 524288 | tf_op jit(solution)/shard_map/all_to_all | solution.py:126
  102.5 30.8 %all-to-all-start.1 = ((bf16[128,2,128]{2,1,0:T(2,128)(2,1)}), bf16[128,2,128]{2,1,0:T(2,128)(2,1)S(1)}, u32[]{:S(2)}, u32[]{:S(2)}) async-start(bf16[128,2,128]{2,1,0:T(2,128)(2,1)} %reshape.696), calls=%async_computation.1 | async-start | bytes 131072 | tf_op jit(solution)/shard_map/all_to_all | solution.py:100
  344.0 11.7 %collective-permute-start.2 = (bf16[1,2,2048]{2,1,0:T(2,128)(2,1)S(1)}, bf16[1,2,2048]{2,1,0:T(2,128)(2,1)S(1)}, u32[]{:S(2)}, u32[]{:S(2)}) collective-permute-start(bf16[1,2,2048]{2,1,0:T(2,128)(2,1)S(1)} %get-tuple-element.291), channel_id=1, source_target_pairs={{0,2},{2,4},{4,6},{6,8},{8,10},{10,12},{12,14},{14,16},{16,18},{18... | collective-permute-start | bytes 24584 | tf_op jit(solution)/shard_map/ppermute | solution.py:21
  346.6 10.4 %collective-permute-start.3 = (bf16[1,2,2048]{2,1,0:T(2,128)(2,1)S(1)}, bf16[1,2,2048]{2,1,0:T(2,128)(2,1)S(1)}, u32[]{:S(2)}, u32[]{:S(2)}) collective-permute-start(bf16[1,2,2048]{2,1,0:T(2,128)(2,1)S(1)} %get-tuple-element.292), channel_id=1, source_target_pairs={{2,0},{4,2},{6,4},{8,6},{10,8},{12,10},{14,12},{16,14},{18,16},{20... | collective-permute-start | bytes 24584 | tf_op jit(solution)/shard_map/ppermute | solution.py:23
where the time goes:
time: 361 us; the launch traced here: 358 us
  matrix products  226 us (63%)
  starting transfers between devices  54.7 us (15%)
  loops' own time  25.6 us (7%)
  blocking collectives  19.9 us (6%)
  waiting for transfers between devices  15.4 us (4%)
  local copies, waits for them, and re-layouts  10.7 us (3%)
  other arithmetic  5.4 us (1%)
    dot_general x4, matrix products, local(): jnp.einsum('kc,wrc->wkr', sin_rows, joined_bf, preferred_element_type=jnp...  33.7 us
    dot_general x4, matrix products, local(): jnp.einsum('kc,wrc->wkr', cos_rows, joined_bf, preferred_element_type=jnp...  32.8 us
    dot_general x4, matrix products, local(): jnp.einsum('wkr,kc->wrc', part_imag, sin_rows, preferred_element_type=jnp...  32.4 us
    dot_general x4, matrix products, local(): jnp.einsum('wkr,kc->wrc', part_real, cos_rows, preferred_element_type=jnp...  31.5 us
    another operation x1, loops' own time, local(): lax.fori_loop(0, total_slots // step_rows, sample_step, (zeros_grid, zero...  25.6 us
    dot_general x3, matrix products, sample_step(): lax.dot_general(sin_rows, flat, (((1,), (1,)), ((), ())), preferred_eleme...  23.8 us
    dot_general x3, matrix products, sample_step(): lax.dot_general(spread, sin_rows, (((0,), (0,)), ((), ())), preferred_ele...  23.6 us
    dot_general x3, matrix products, sample_step(): lax.dot_general(cos_rows, flat, (((1,), (1,)), ((), ())), preferred_eleme...  23.5 us
  transfers between devices with their start and end apart: 6, of which 2 were waited for; matrix products, arithmetic and copies ran while one was open for 21% of the time, Pallas kernels for 0%

commit v1 on v0

v1 whole, which is shorter than its diff:
```python
import math

import jax
import jax.numpy as jnp
import numpy as np
from jax import lax
from jax.experimental import pallas as pl
from jax.experimental.pallas import tpu as pltpu
from jax.sharding import PartitionSpec as P

F32 = jnp.float32
BF16 = jnp.bfloat16
NT = (((1,), (1,)), ((), ()))
NN = (((1,), (0,)), ((), ()))
fields = 8
halo = 4


def angle(first, second, length):
    turn = (np.outer(first, second) % length) * (2.0 * math.pi / length)
    return np.cos(turn), np.sin(turn)


def tables(rows, slabs, owned, grid):
    fine = grid // slabs
    lanes = owned * rows
    c2, k2, k1 = np.arange(slabs), np.arange(slabs // 2), np.arange(fine)
    cos, sin = angle(k2, c2, slabs)
    row_forward = np.block([[cos, sin], [-sin, cos]])
    row_back = np.block([[cos, sin], [-sin, cos]])
    col_turn = angle(k1, c2, grid)
    cos, sin = angle(c2, c2, slabs)
    coarse = np.block([[cos, sin], [-sin, cos]])
    cos, sin = angle(k1, k1, fine)
    eye = np.eye(owned)
    cos, sin = np.kron(eye, cos), np.kron(eye, sin)
    inner = np.block([[cos, -sin], [sin, cos]])
    row_turn = [np.tile(part, (1, owned)) for part in angle(c2, k1, grid)]
    low = [row_forward, row_back, coarse, coarse.T, inner, inner.T]
    high = [*col_turn, *row_turn]
    assert lanes == slabs
    return [jnp.asarray(t, BF16) for t in low], [jnp.asarray(t, F32) for t in high]


def payload_kernel(row, block, column, real, imag, weight, out, wide):
    vis_count = row.shape[1]
    slabs = out.shape[0]
    hot = (
        lax.broadcasted_iota(jnp.int32, (slabs, vis_count), 0) == block[...]
    ).astype(F32)
    hot_low = hot.astype(BF16)
    earlier = (
        lax.broadcasted_iota(jnp.int32, (vis_count, vis_count), 0)
        < lax.broadcasted_iota(jnp.int32, (vis_count, vis_count), 1)
    ).astype(F32).astype(BF16)
    before = lax.dot_general(hot_low, earlier, NN, preferred_element_type=F32)
    rank = jnp.sum(before * hot, axis=0, keepdims=True)
    ky = row[...]
    parts = [
        jnp.bitwise_and(ky, slabs - 1).astype(F32),
        (column[...] * (slabs // 8) + ky // slabs).astype(F32),
    ]
    for value in (real, imag, weight):
        whole = value[...]
        lead = whole.astype(BF16).astype(F32)
        parts += [lead, whole - lead]
    which = lax.broadcasted_iota(jnp.int32, (fields, vis_count), 0)
    stack = jnp.zeros((fields, vis_count), F32)
    for index, part in enumerate(parts):
        stack = jnp.where(which == index, part, stack)
    for slot in range(slabs // fields):
        wide[slot * fields : (slot + 1) * fields, :] = jnp.where(
            rank == float(slot), stack, 0.0
        )
    out[...] = lax.dot_general(
        hot_low, wide[...].astype(BF16), NT, preferred_element_type=F32
    )


def lane_roll(x, shift):
    return pltpu.roll(x, shift % x.shape[1], 1)


def row_roll(x, shift):
    return pltpu.roll(x, shift % x.shape[0], 0)


def slope(x, roll):
    return (8.0 * (roll(x, -1) - roll(x, 1)) - (roll(x, -2) - roll(x, 2))) * (1.0 / 12.0)


def cosine(index, length):
    return math.cos(2.0 * math.pi * (index % length) / length)


def sine(index, length):
    return math.sin(2.0 * math.pi * (index % length) / length)


def weighted(terms):
    total = None
    for factor, value in terms:
        if abs(factor) < 1e-12:
            continue
        if abs(factor - 1.0) < 1e-12:
            term = value
        elif abs(factor + 1.0) < 1e-12:
            term = -value
        else:
            term = factor * value
        total = term if total is None else total + term
    return total


def spectrum_kernel(
    screen, image, before, after, pay, table, turn_cos, turn_sin,
    out, slope_x, slope_y, frame, other, folded, packed,
):
    rows, grid = image.shape
    fine = turn_cos.shape[0]
    width = turn_cos.shape[1]
    low = before[...].astype(F32)
    high = after[...].astype(F32)
    frame[0:halo, :] = low[0:halo]
    frame[halo : halo + rows, :] = image[...]
    frame[halo + rows :, :] = high[0:halo]
    other[0:halo, :] = low[halo:]
    other[halo : halo + rows, :] = screen[...]
    other[halo + rows :, :] = high[halo:]
    image_y = slope(frame[...], row_roll)
    slope_y[...] = image_y
    image_x = slope(image[...], lane_roll)
    slope_x[...] = image_x
    change_y = slope(other[...], row_roll) * image_y
    other[...] = change_y
    joined = (
        image[...]
        + slope(screen[...], lane_roll) * image_x
        + other[halo : halo + rows, :]
    )
    tiles = [joined[:, i * width : (i + 1) * width] for i in range(fine)]
    half = fine // 2
    even = [tiles[j] + tiles[fine - j] for j in range(1, half)]
    odd = [tiles[j] - tiles[fine - j] for j in range(1, half)]
    for k in range(half + 1):
        part_real = weighted(
            [(1.0, tiles[0]), ((-1.0) ** k, tiles[half])]
            + [(cosine(j * k, fine), even[j - 1]) for j in range(1, half)]
        )
        part_imag = weighted([(-sine(j * k, fine), odd[j - 1]) for j in range(1, half)])
        for index in sorted({k, (fine - k) % fine}):
            sign = 1.0 if index == k else -1.0
            cos = turn_cos[index : index + 1, :]
            sin = turn_sin[index : index + 1, :]
            lead, trail = part_real * cos, part_real * sin
            if part_imag is None:
                value_real, value_imag = lead, -trail
            else:
                value_real = lead + sign * (part_imag * sin)
                value_imag = sign * (part_imag * cos) - trail
            span = slice(index * rows, (index + 1) * rows)
            folded[span, 0:width] = value_real.astype(BF16)
            folded[span, width:] = value_imag.astype(BF16)
    spectrum = lax.dot_general(table[...], folded[...], NT, preferred_element_type=F32)
    deep = width // 2
    for side in range(2):
        for part in range(2):
            packed[pl.ds(side * 4 + part, deep, stride=8), :] = spectrum[
                part * deep : (part + 1) * deep, side * width : (side + 1) * width
            ]
    packed[pl.ds(2, width, stride=4), :] = pay[...]
    packed[pl.ds(3, width, stride=4), :] = jnp.zeros((width, width), F32)
    out[...] = packed[...].astype(BF16)


def visibility_kernel(
    arrived, coarse, coarse_back, inner, inner_back, turn_cos, turn_sin,
    out, wide, hot, hot_back, spread, *, slots, scale,
):
    width = arrived.shape[1]
    wide[...] = arrived[...].astype(F32)
    part_real = wide[pl.ds(0, width, stride=4), :]
    part_imag = wide[pl.ds(1, width, stride=4), :]
    pay = wide[pl.ds(2, width, stride=4), :]
    pay_back = jnp.transpose(pay)
    stacked = jnp.concatenate([part_real, part_imag], 0).astype(BF16)
    mixed = lax.dot_general(coarse[...], stacked, NN, preferred_element_type=F32)
    cos, sin = turn_cos[...], turn_sin[...]
    left, right = mixed[:width], mixed[width:]
    turned = jnp.concatenate([left * cos + right * sin, right * cos - left * sin], 1)
    cells = scale * lax.dot_general(
        turned.astype(BF16), inner[...], NN, preferred_element_type=F32
    )
    lead = cells.astype(BF16)
    rest = (cells - lead.astype(F32)).astype(BF16)
    across = lax.broadcasted_iota(jnp.int32, (width, width), 1).astype(F32)
    down = lax.broadcasted_iota(jnp.int32, (width, width), 0).astype(F32)
    for slot in range(slots):
        at = slot * fields
        span = slice(slot * width, (slot + 1) * width)
        hot[span, :] = (pay[:, at : at + 1] == across).astype(F32).astype(BF16)
        hot_back[:, span] = (pay_back[at : at + 1, :] == down).astype(F32).astype(BF16)
    picked = lax.dot_general(
        hot[...], lead, NN, preferred_element_type=F32
    ) + lax.dot_general(hot[...], rest, NN, preferred_element_type=F32)
    for slot in range(slots):
        at = slot * fields
        span = slice(slot * width, (slot + 1) * width)
        value = [pay[:, at + i : at + i + 1] for i in range(fields)]
        mask = value[1] == across
        weight = value[6] + value[7]
        for part in range(2):
            model = jnp.sum(
                jnp.where(mask, picked[span, part * width : (part + 1) * width], 0.0),
                axis=1,
                keepdims=True,
            )
            error = weight * (model - (value[2 + 2 * part] + value[3 + 2 * part]))
            spread[span, part * width : (part + 1) * width] = jnp.where(
                mask, error, 0.0
            ).astype(BF16)
    sums = lax.dot_general(hot_back[...], spread[...], NN, preferred_element_type=F32)
    mixed = lax.dot_general(
        sums.astype(BF16), inner_back[...], NN, preferred_element_type=F32
    )
    left, right = mixed[:, :width], mixed[:, width:]
    turned = jnp.concatenate([left * cos - right * sin, right * cos + left * sin], 0)
    back = lax.dot_general(
        coarse_back[...], turned.astype(BF16), NN, preferred_element_type=F32
    )
    fine = 16
    place = jnp.bitwise_and(
        lax.broadcasted_iota(jnp.int32, (width, width), 1), fine - 1
    )
    for part in range(2):
        own = back[part * width : (part + 1) * width]
        wide[pl.ds(part, width, stride=4), :] = own
        wide[pl.ds(2 + part, width, stride=4), :] = jnp.where(
            place >= fine - 2, row_roll(own, 1), jnp.where(place < 2, row_roll(own, -1), 0.0)
        )
    out[...] = wide[...].astype(BF16)


def gradient_kernel(
    arrived, slope_x, slope_y, table, turn_cos, turn_sin,
    out, wide, grouped, frame, *, scale,
):
    rows, grid = slope_x.shape
    fine, width = turn_cos.shape
    deep = width // 2
    half = fine // 2
    wide[...] = arrived[...].astype(F32)
    frame[...] = jnp.zeros(frame.shape, F32)
    main = None
    for kind in (1, 0):
        for side in range(2):
            for part in range(2):
                grouped[
                    part * deep : (part + 1) * deep, side * width : (side + 1) * width
                ] = wide[pl.ds(side * 4 + 2 * kind + part, deep, stride=8), :]
        flat = jnp.transpose(grouped[...]).astype(BF16)
        spread = lax.dot_general(flat, table[...], NN, preferred_element_type=F32)
        real, imag = [], []
        for k in range(fine):
            cos = scale * turn_cos[k : k + 1, :]
            sin = scale * turn_sin[k : k + 1, :]
            left = spread[k * rows : (k + 1) * rows, 0:width]
            right = spread[k * rows : (k + 1) * rows, width:]
            real.append(left * cos - right * sin)
            imag.append(right * cos + left * sin)
        even = [real[k] + real[fine - k] for k in range(1, half)]
        odd = [imag[k] - imag[fine - k] for k in range(1, half)]
        for c in range(half + 1):
            plain = weighted(
                [(1.0, real[0]), ((-1.0) ** c, real[half])]
                + [(cosine(c * k, fine), even[k - 1]) for k in range(1, half)]
            )
            cross = weighted([(sine(c * k, fine), odd[k - 1]) for k in range(1, half)])
            for index in sorted({c, (fine - c) % fine}):
                if cross is None:
                    value = plain
                else:
                    value = plain - cross if index == c else plain + cross
                span = slice(index * width, (index + 1) * width)
                if kind == 1:
                    frame[halo - 2 : halo, span] = value[rows - 2 :]
                    frame[halo + rows : halo + rows + 2, span] = value[0:2]
                else:
                    frame[halo : halo + rows, span] = value
    push_x = frame[halo : halo + rows, :] * slope_x[...]
    frame[...] = -slope(frame[...] * slope_y[...], row_roll)
    out[...] = frame[halo : halo + rows, :] - slope(push_x, lane_roll)


def whole(count):
    return [pl.BlockSpec(memory_space=pltpu.VMEM)] * count


def local(screens, image, vis_row, vis_block, vis_column, vis_real, vis_imag, vis_weight):
    rows, grid = image.shape
    slabs = lax.axis_size("slab")
    owned = grid // 2 // slabs
    slots = 3 * vis_row.shape[0] // slabs
    screen = screens.reshape(rows, grid)
    low, high = tables(rows, slabs, owned, grid)
    row_forward, row_back, coarse, coarse_back, inner, inner_back = low
    col_cos, col_sin, row_cos, row_sin = high
    width = slabs

    ring = [(i, (i + 1) % slabs) for i in range(slabs)]
    tail = jnp.concatenate([image[rows - halo :], screen[rows - halo :]], 0).astype(BF16)
    head = jnp.concatenate([image[:halo], screen[:halo]], 0).astype(BF16)
    before = lax.ppermute(tail, "slab", ring)
    after = lax.ppermute(head, "slab", [(b, a) for a, b in ring])

    line = (1, vis_row.shape[0])
    pay = pl.pallas_call(
        payload_kernel,
        out_shape=jax.ShapeDtypeStruct((slabs, width), F32),
        in_specs=whole(6),
        out_specs=pl.BlockSpec(memory_space=pltpu.VMEM),
        scratch_shapes=[pltpu.VMEM((width, line[1]), F32)],
        cost_estimate=pl.CostEstimate(flops=30_000_000, bytes_accessed=200_000, transcendentals=0),
        name="payload",
    )(
        vis_row.reshape(line), vis_block.reshape(line), vis_column.reshape(line),
        vis_real.reshape(line), vis_imag.reshape(line), vis_weight.reshape(line),
    )
    framed = rows + 2 * halo
    send, slope_x, slope_y = pl.pallas_call(
        spectrum_kernel,
        out_shape=[
            jax.ShapeDtypeStruct((4 * slabs, width), BF16),
            jax.ShapeDtypeStruct((rows, grid), F32),
            jax.ShapeDtypeStruct((framed, grid), F32),
        ],
        in_specs=whole(8),
        out_specs=whole(3),
        scratch_shapes=[
            pltpu.VMEM((framed, grid), F32),
            pltpu.VMEM((framed, grid), F32),
            pltpu.VMEM((2 * width, 2 * width), BF16),
            pltpu.VMEM((4 * slabs, width), F32),
        ],
        name="spectrum",
    )(screen, image, before, after, pay, row_forward, col_cos, col_sin)
    arrived = lax.all_to_all(
        send.reshape(slabs, 4, width), "slab", split_axis=0, concat_axis=0, tiled=True
    ).reshape(4 * slabs, width)
    scale = 1.0 / grid
    back = pl.pallas_call(
        lambda *refs: visibility_kernel(*refs, slots=slots, scale=scale),
        out_shape=jax.ShapeDtypeStruct((4 * slabs, width), BF16),
        in_specs=whole(7),
        out_specs=pl.BlockSpec(memory_space=pltpu.VMEM),
        scratch_shapes=[
            pltpu.VMEM((4 * slabs, width), F32),
            pltpu.VMEM((slots * width, width), BF16),
            pltpu.VMEM((width, slots * width), BF16),
            pltpu.VMEM((slots * width, 2 * width), BF16),
        ],
        name="visibility",
    )(arrived, coarse, coarse_back, inner, inner_back, row_cos, row_sin)
    returned = lax.all_to_all(
        back.reshape(slabs, 4, width), "slab", split_axis=0, concat_axis=0, tiled=True
    ).reshape(4 * slabs, width)
    grad = pl.pallas_call(
        lambda *refs: gradient_kernel(*refs, scale=scale),
        out_shape=jax.ShapeDtypeStruct((rows, grid), F32),
        in_specs=whole(6),
        out_specs=pl.BlockSpec(memory_space=pltpu.VMEM),
        scratch_shapes=[
            pltpu.VMEM((4 * slabs, width), F32),
            pltpu.VMEM((width, 2 * width), F32),
            pltpu.VMEM((framed, grid), F32),
        ],
        name="gradient",
    )(returned, slope_x, slope_y, row_back, col_cos, col_sin)
    return grad.reshape(1, rows, grid)


def solution(mesh):
    in_specs = (
        P(("chain", "vis"), "slab", None),
        P(("chain", "slab"), None),
        P("slab"),
        P("slab", None),
        P("slab"),
        P("slab"),
        P("slab"),
        P("slab"),
    )
    out_specs = P(("chain", "vis"), "slab", None)
    return jax.shard_map(local, mesh=mesh, in_specs=in_specs, out_specs=out_specs, check_vma=False)
```

time: 361 us -> 78.6 us (0.22)
  matrix products: 226 us -> 0 us
  starting transfers between devices: 54.7 us -> 17.3 us
  blocking collectives: 19.9 us -> 48.3 us
  loops' own time: 25.6 us -> 0 us
  waiting for transfers between devices: 15.4 us -> 0.01 us
  Pallas kernels: 0 us -> 10.8 us
  local copies, waits for them, and re-layouts: 10.7 us -> 0.64 us
  other arithmetic: 5.4 us -> 1 us
    dot_general x29 -> x0, matrix products: 226 us -> none  [the longest x4 33.7 us: local(): jnp.einsum('kc,wrc->wkr', sin_rows, joined_bf, preferred_element_type=jnp...]
    all_to_all x1 -> x2, blocking collectives: 19.9 us -> 48.3 us  [the longest x1 26.4 us: local(): lax.all_to_all(send.reshape(slabs, 4, width), 'slab', split_axis=0, conca...]
    all_to_all x2 -> x0, starting transfers between devices: 25.8 us -> none  [the longest x1 16.4 us: local(): lax.all_to_all(spectra, 'slab', split_axis=2, concat_axis=3, tiled=True)]
    another operation x1 -> x0, loops' own time: 25.6 us -> none  [local(): lax.fori_loop(0, total_slots // step_rows, sample_step, (zeros_grid, zero...]
    all_to_all x2 -> x0, waiting for transfers between devices: 14.1 us -> none  [the longest x1 14.1 us: local(): lax.all_to_all(spectra, 'slab', split_axis=2, concat_axis=3, tiled=True)]
    ppermute x4 -> x2, starting transfers between devices: 28.9 us -> 17.3 us  [the longest x1 13.8 us: local(): after = lax.ppermute(head, 'slab', [(b, a) for a, b in ring])]
    pallas_call x0 -> x4, Pallas kernels: none -> 10.8 us  [the longest x1 4.24 us: local(): pl.pallas_call(lambda *refs: visibility_kernel(*refs, slots=slots, scale=...]
  transfers between devices with their start and end apart: 6 -> 2, of which waited for: 2 -> 0; matrix products, arithmetic and copies ran while one was open for 21% -> 0% of each run, Pallas kernels for 0% -> 2%
where the time goes in v1:
time: 78.6 us; the launch traced here: 78.3 us
  blocking collectives  48.3 us (61%)
  starting transfers between devices  17.3 us (22%)
  Pallas kernels  10.8 us (14%)
  other arithmetic  1 us (1%)
    all_to_all x1, blocking collectives, local(): lax.all_to_all(send.reshape(slabs, 4, width), 'slab', split_axis=0, conca...  26.4 us
    all_to_all x1, blocking collectives, local(): lax.all_to_all(back.reshape(slabs, 4, width), 'slab', split_axis=0, conca...  22 us
    ppermute x1, starting transfers between devices, local(): after = lax.ppermute(head, 'slab', [(b, a) for a, b in ring])  13.8 us
    pallas_call x1, Pallas kernels, local(): pl.pallas_call(lambda *refs: visibility_kernel(*refs, slots=slots, scale=...  4.24 us
    ppermute x1, starting transfers between devices, local(): before = lax.ppermute(tail, 'slab', ring)  3.48 us
    pallas_call x1, Pallas kernels, local(): pl.pallas_call(lambda *refs: gradient_kernel(*refs, scale=scale), out_sha...  2.45 us
    pallas_call x1, Pallas kernels, local(): pl.pallas_call(spectrum_kernel, out_shape=[jax.ShapeDtypeStruct((4 * slab...  2.41 us
    pallas_call x1, Pallas kernels, local(): pl.pallas_call(payload_kernel, out_shape=jax.ShapeDtypeStruct((slabs, wid...  1.75 us
  transfers between devices with their start and end apart: 2, of which 0 were waited for; matrix products, arithmetic and copies ran while one was open for 0% of the time, Pallas kernels for 2%

profile of v1, /device:TPU:2, one launch (start us, length us, event | category | flops | bytes accessed | tf_op | source)
XLA Modules:
  0.0 78.3 jit_solution(6116319101219838571)
XLA Ops:
  0.0 0.0 copy-start
  0.0 0.9 %convert.15 = bf16[1,16,2048]{2,1,0:T(8,128)(2,1)S(1)} convert(f32[1,16,2048]{2,1,0:T(8,128)} %param.18) | non-fusion elementwise | flops 32768 | bytes 196608 | tf_op jit(solution)/shard_map/convert.8
  1.0 0.0 copy-done
  1.1 3.5 %collective-permute-start = (bf16[8,2048]{1,0:T(8,128)(2,1)S(1)}, bf16[8,2048]{1,0:T(8,128)(2,1)S(1)}, u32[]{:S(2)}, u32[]{:S(2)}) collective-permute-start(bf16[8,2048]{1,0:T(8,128)(2,1)S(1)} %pad_maximum_fusion), channel_id=1, source_target_pairs={{0,2},{2,4},{4,6},{6,8},{8,10},{10,12},{12,14},{14,16},{16,18},{18... | collective-permute-start | bytes 98312 | tf_op jit(solution)/shard_map/ppermute | solution.py:313
  4.6 13.8 %collective-permute-start.1 = (bf16[8,2048]{1,0:T(8,128)(2,1)S(1)}, bf16[8,2048]{1,0:T(8,128)(2,1)S(1)}, u32[]{:S(2)}, u32[]{:S(2)}) collective-permute-start(bf16[8,2048]{1,0:T(8,128)(2,1)S(1)} %pad_maximum_fusion.1), channel_id=1, source_target_pairs={{2,0},{4,2},{6,4},{8,6},{10,8},{12,10},{14,12},{16,14},{18,16},{20... | collective-permute-start | bytes 98312 | tf_op jit(solution)/shard_map/ppermute | solution.py:314
  18.4 1.8 %payload.1.pay = f32[128,128]{1,0:T(8,128)} custom-call(s32[1,256]{1,0:T(1,128)} %bitcast.21, s32[1,256]{1,0:T(1,128)} %bitcast.22, s32[1,256]{1,0:T(1,128)} %bitcast.23, f32[1,256]{1,0:T(1,128)} %bitcast.24, f32[1,256]{1,0:T(1,128)} %bitcast.25, f32[1,256]{1,0:T(1,128)} %bitcast.26), custom_call_target="tpu_custom_call" | custom-call | flops 30000000 | bytes 200000 | tf_op jit(solution)/shard_map/payload/pallas_call | solution.py:317
  20.2 0.0 collective-permute-done.before
  20.2 0.0 copy-start.1
  20.2 0.0 collective-permute-done.1.after
  20.2 0.0 copy-start.2
  20.2 0.6 copy-done.1
  20.8 0.0 copy-done.2
  20.8 2.4 %spectrum.1 = (bf16[512,128]{1,0:T(8,128)(2,1)}, f32[16,2048]{1,0:T(8,128)}, f32[24,2048]{1,0:T(8,128)}) custom-call(f32[16,2048]{1,0:T(8,128)} %bitcast.18, f32[16,2048]{1,0:T(8,128)} %image.1, bf16[8,2048]{1,0:T(8,128)(2,1)} %copy-done.1, bf16[8,2048]{1,0:T(8,128)(2,1)} %copy-done.2, f32[128,128]{1,0:T(8,128)} %payload.1.pay, ...), custom_call_target="tpu_custom_call" | custom-call | tf_op jit(solution)/shard_map/spectrum/pallas_call | solution.py:330
  23.2 26.4 %all_to_all.10 = bf16[128,4,128]{2,1,0:T(4,128)(2,1)} all-to-all(bf16[128,4,128]{2,1,0:T(4,128)(2,1)} %bitcast.20), channel_id=1, replica_groups=mesh['chain'=2,'slab'=128,'vis'=2] {'slab'}, dimensions={0} | all-to-all | bytes 262144 | tf_op jit(solution)/shard_map/all_to_all | solution.py:347
  49.6 4.2 %visibility.1 = bf16[512,128]{1,0:T(8,128)(2,1)} custom-call(bf16[512,128]{1,0:T(8,128)(2,1)} %bitcast.16, bf16[256,256]{1,0:T(8,128)(2,1)} %constant.19.clone.refs_1_, bf16[256,256]{1,0:T(8,128)(2,1)} %constant.20.clone.refs_2_, bf16[256,256]{1,0:T(8,128)(2,1)} %constant.21.clone.refs_3_, bf16[256,256]{1,0:T(8,128)(2,1)} %constant.22.clone.refs_4_, ...), custom_call_target="tpu_custom_call" | custom-call | tf_op jit(solution)/shard_map/visibility/pallas_call | solution.py:351
  53.8 22.0 %all_to_all.11 = bf16[128,4,128]{2,1,0:T(4,128)(2,1)} all-to-all(bf16[128,4,128]{2,1,0:T(4,128)(2,1)} %bitcast.17), channel_id=1, replica_groups=mesh['chain'=2,'slab'=128,'vis'=2] {'slab'}, dimensions={0} | all-to-all | bytes 262144 | tf_op jit(solution)/shard_map/all_to_all | solution.py:364
  75.8 2.4 %gradient.1 = f32[16,2048]{1,0:T(8,128)} custom-call(bf16[512,128]{1,0:T(8,128)(2,1)} %bitcast.19, f32[16,2048]{1,0:T(8,128)} %get-tuple-element.9.refs_1_, f32[24,2048]{1,0:T(8,128)} %get-tuple-element.10.refs_2_, bf16[128,256]{1,0:T(8,128)(2,1)} %constant.18.clone.table.refs_3_, f32[16,128]{1,0:T(8,128)} %constant.23.clone.turn_cos.refs_4_, ...), custom_call_target="tpu_custom_call" | custom-call | tf_op jit(solution)/shard_map/gradient/pallas_call | solution.py:367
  (5 shorter events, 0.1 us)
Async XLA Ops:
  0.0 1.0 %copy-start = (f32[16,2048]{1,0:T(8,128)S(1)}, f32[16,2048]{1,0:T(8,128)}, u32[]{:S(2)}) copy-start(f32[16,2048]{1,0:T(8,128)} %image.1) | copy-start | bytes 393220
  1.1 19.1 %collective-permute-start = (bf16[8,2048]{1,0:T(8,128)(2,1)S(1)}, bf16[8,2048]{1,0:T(8,128)(2,1)S(1)}, u32[]{:S(2)}, u32[]{:S(2)}) collective-permute-start(bf16[8,2048]{1,0:T(8,128)(2,1)S(1)} %pad_maximum_fusion), channel_id=1, source_target_pairs={{0,2},{2,4},{4,6},{6,8},{8,10},{10,12},{12,14},{14,16},{16,18},{18... | collective-permute-start | bytes 98312 | tf_op jit(solution)/shard_map/ppermute | solution.py:313
  4.6 15.6 %collective-permute-start.1 = (bf16[8,2048]{1,0:T(8,128)(2,1)S(1)}, bf16[8,2048]{1,0:T(8,128)(2,1)S(1)}, u32[]{:S(2)}, u32[]{:S(2)}) collective-permute-start(bf16[8,2048]{1,0:T(8,128)(2,1)S(1)} %pad_maximum_fusion.1), channel_id=1, source_target_pairs={{2,0},{4,2},{6,4},{8,6},{10,8},{12,10},{14,12},{16,14},{18,16},{20... | collective-permute-start | bytes 98312 | tf_op jit(solution)/shard_map/ppermute | solution.py:314
  20.2 0.6 copy-start.1
  20.2 0.6 copy-start.2

commit v2 on v1

v2 whole, which is shorter than its diff:
```python
import math

import jax
import jax.numpy as jnp
import numpy as np
from jax import lax
from jax.experimental import pallas as pl
from jax.experimental.pallas import tpu as pltpu
from jax.sharding import PartitionSpec as P

F32 = jnp.float32
BF16 = jnp.bfloat16
NT = (((1,), (1,)), ((), ()))
NN = (((1,), (0,)), ((), ()))
fields = 8
halo = 4
lead = 2


def angle(first, second, length):
    turn = (np.outer(first, second) % length) * (2.0 * math.pi / length)
    return np.cos(turn), np.sin(turn)


def tables(rows, slabs, owned, grid):
    fine = grid // slabs
    c2, k2, k1 = np.arange(slabs), np.arange(slabs // 2), np.arange(fine)
    shifted = np.arange(rows) - lead
    cos, sin = angle(k2, c2, slabs)
    row_forward = np.block([[cos, sin], [-sin, cos]])
    row_back = np.block([[cos, sin], [-sin, cos]])
    col_turn = angle(k1, c2, grid)
    cos, sin = angle(c2, c2, slabs)
    coarse = np.block([[cos, sin], [-sin, cos]])
    cos, sin = angle(shifted, k1, fine)
    eye = np.eye(owned)
    cos, sin = np.kron(eye, cos), np.kron(eye, sin)
    inner = np.block([[cos, -sin], [sin, cos]])
    row_turn = [np.tile(part, (1, owned)) for part in angle(c2, shifted, grid)]
    low = [row_forward, row_back, coarse, coarse.T, inner, inner.T]
    high = [*col_turn, *row_turn]
    return [jnp.asarray(t, BF16) for t in low], [jnp.asarray(t, F32) for t in high]


def payload_kernel(row, block, column, real, imag, weight, out, wide):
    vis_count = row.shape[1]
    slabs = out.shape[0]
    hot = (
        lax.broadcasted_iota(jnp.int32, (slabs, vis_count), 0) == block[...]
    ).astype(F32)
    hot_low = hot.astype(BF16)
    earlier = (
        lax.broadcasted_iota(jnp.int32, (vis_count, vis_count), 0)
        < lax.broadcasted_iota(jnp.int32, (vis_count, vis_count), 1)
    ).astype(F32).astype(BF16)
    before = lax.dot_general(hot_low, earlier, NN, preferred_element_type=F32)
    rank = jnp.sum(before * hot, axis=0, keepdims=True)
    ky = row[...]
    parts = [
        jnp.bitwise_and(ky, slabs - 1).astype(F32),
        (column[...] * (slabs // 8) + ky // slabs).astype(F32),
    ]
    for value in (real, imag, weight):
        whole = value[...]
        lead = whole.astype(BF16).astype(F32)
        parts += [lead, whole - lead]
    which = lax.broadcasted_iota(jnp.int32, (fields, vis_count), 0)
    stack = jnp.zeros((fields, vis_count), F32)
    for index, part in enumerate(parts):
        stack = jnp.where(which == index, part, stack)
    for slot in range(slabs // fields):
        wide[slot * fields : (slot + 1) * fields, :] = jnp.where(
            rank == float(slot), stack, 0.0
        )
    out[...] = lax.dot_general(
        hot_low, wide[...].astype(BF16), NT, preferred_element_type=F32
    )


def lane_roll(x, shift):
    return pltpu.roll(x, shift % x.shape[1], 1)


def row_roll(x, shift):
    return pltpu.roll(x, shift % x.shape[0], 0)


def slope(x, roll):
    return (8.0 * (roll(x, -1) - roll(x, 1)) - (roll(x, -2) - roll(x, 2))) * (1.0 / 12.0)


def cosine(index, length):
    return math.cos(2.0 * math.pi * (index % length) / length)


def sine(index, length):
    return math.sin(2.0 * math.pi * (index % length) / length)


def weighted(terms):
    total = None
    for factor, value in terms:
        if abs(factor) < 1e-12:
            continue
        if abs(factor - 1.0) < 1e-12:
            term = value
        elif abs(factor + 1.0) < 1e-12:
            term = -value
        else:
            term = factor * value
        total = term if total is None else total + term
    return total


def spectrum_kernel(
    screen, image, before, pay, table, turn_cos, turn_sin,
    out, slope_x, slope_y, frame, other, folded, packed, relayed,
):
    rows, grid = image.shape
    fine, width = turn_cos.shape
    framed = frame.shape[0]
    edge = before[...].astype(F32)
    for index, (ref, own) in enumerate(((frame, image), (other, screen))):
        part = edge[index * halo : (index + 1) * halo]
        ref[0:lead, :] = part[halo - lead :]
        ref[lead : lead + rows, :] = own[...]
        ref[lead + rows : framed - lead, :] = jnp.zeros((framed - rows - 2 * lead, grid), F32)
        ref[framed - lead :, :] = part[: halo - lead]
    field = frame[...]
    image_x = slope(field, lane_roll)
    image_y = slope(field, row_roll)
    slope_x[...] = row_roll(image_x, -lead)[0:rows]
    slope_y[...] = image_y[0:rows]
    for i in range(fine):
        relayed[i * 8 : (i + 1) * 8, :] = image_y[0:8, i * width : (i + 1) * width]
    change = other[...]
    change_x = slope(change[0:rows], lane_roll) * image_x[0:rows]
    joined = field[0:rows] + change_x + (slope(change, row_roll) * image_y)[0:rows]
    tiles = [joined[:, i * width : (i + 1) * width] for i in range(fine)]
    half = fine // 2
    even = [tiles[j] + tiles[fine - j] for j in range(1, half)]
    odd = [tiles[j] - tiles[fine - j] for j in range(1, half)]
    for k in range(half + 1):
        part_real = weighted(
            [(1.0, tiles[0]), ((-1.0) ** k, tiles[half])]
            + [(cosine(j * k, fine), even[j - 1]) for j in range(1, half)]
        )
        part_imag = weighted([(-sine(j * k, fine), odd[j - 1]) for j in range(1, half)])
        for index in sorted({k, (fine - k) % fine}):
            sign = 1.0 if index == k else -1.0
            cos = turn_cos[index : index + 1, :]
            sin = turn_sin[index : index + 1, :]
            first, second = part_real * cos, part_real * sin
            if part_imag is None:
                value_real, value_imag = first, -second
            else:
                value_real = first + sign * (part_imag * sin)
                value_imag = sign * (part_imag * cos) - second
            span = slice(index * rows, (index + 1) * rows)
            folded[span, 0:width] = value_real.astype(BF16)
            folded[span, width:] = value_imag.astype(BF16)
    spectrum = lax.dot_general(table[...], folded[...], NT, preferred_element_type=F32)
    deep = width // 2
    for side in range(2):
        for part in range(2):
            packed[pl.ds(side * 4 + part, deep, stride=8), :] = spectrum[
                part * deep : (part + 1) * deep, side * width : (side + 1) * width
            ]
    packed[pl.ds(2, width, stride=4), :] = pay[...]
    packed[pl.ds(3, width, stride=4), :] = jnp.transpose(relayed[...])
    out[...] = packed[...].astype(BF16)


def visibility_kernel(
    arrived, coarse, coarse_back, inner, inner_back, turn_cos, turn_sin,
    out, wide, hot, spread, *, slots, scale,
):
    width = arrived.shape[1]
    wide[...] = arrived[...].astype(F32)
    part_real = wide[pl.ds(0, width, stride=4), :]
    part_imag = wide[pl.ds(1, width, stride=4), :]
    pay = jnp.transpose(wide[pl.ds(2, width, stride=4), :])
    relayed = wide[pl.ds(3, width, stride=4), :]
    stacked = jnp.concatenate([part_real, part_imag], 0).astype(BF16)
    mixed = lax.dot_general(coarse[...], stacked, NN, preferred_element_type=F32)
    cos, sin = turn_cos[...], turn_sin[...]
    left, right = mixed[:width], mixed[width:]
    turned = jnp.concatenate([left * cos + right * sin, right * cos - left * sin], 1)
    cells = scale * jnp.transpose(
        lax.dot_general(turned.astype(BF16), inner[...], NN, preferred_element_type=F32)
    )
    main = cells.astype(BF16)
    rest = (cells - main.astype(F32)).astype(BF16)
    split = jnp.concatenate([main, rest], 1)
    down = lax.broadcasted_iota(jnp.int32, (width, width), 0).astype(F32)
    for slot in range(slots):
        at = slot * fields
        span = slice(slot * width, (slot + 1) * width)
        one = (pay[at : at + 1, :] == down).astype(F32).astype(BF16)
        hot[0:width, span] = one
        hot[width:, span] = one
    picked = lax.dot_general(split, hot[...], NN, preferred_element_type=F32)
    for slot in range(slots):
        at = slot * fields
        span = slice(slot * width, (slot + 1) * width)
        value = [pay[at + i : at + i + 1, :] for i in range(fields)]
        mask = value[1] == down
        weight = value[6] + value[7]
        for part in range(2):
            model = jnp.sum(
                jnp.where(mask, picked[part * width : (part + 1) * width, span], 0.0),
                axis=0,
                keepdims=True,
            )
            error = weight * (model - (value[2 + 2 * part] + value[3 + 2 * part]))
            spread[part * width : (part + 1) * width, span] = jnp.where(
                mask, error, 0.0
            ).astype(BF16)
    sums = lax.dot_general(
        hot[0:width, :], spread[...], NT, preferred_element_type=F32
    )
    mixed = lax.dot_general(
        sums.astype(BF16), inner_back[...], NN, preferred_element_type=F32
    )
    left, right = mixed[:, :width], mixed[:, width:]
    turned = jnp.concatenate([left * cos - right * sin, right * cos + left * sin], 0)
    back = lax.dot_general(
        coarse_back[...], turned.astype(BF16), NN, preferred_element_type=F32
    )
    place = jnp.bitwise_and(lax.broadcasted_iota(jnp.int32, (width, width), 1), 15)
    real, imag = back[:width], back[width:]
    wide[pl.ds(0, width, stride=4), :] = real
    wide[pl.ds(1, width, stride=4), :] = imag
    wide[pl.ds(2, width, stride=4), :] = jnp.where(
        place < 8, row_roll(real, -1), lane_roll(row_roll(imag, -1), 8)
    )
    wide[pl.ds(3, width, stride=4), :] = row_roll(relayed, -1)
    out[...] = wide[...].astype(BF16)


def gradient_kernel(
    arrived, slope_x, slope_y, table, turn_cos, turn_sin,
    out, wide, grouped, push_x, *, scale,
):
    rows, grid = slope_x.shape
    fine, width = turn_cos.shape
    deep = width // 2
    half = fine // 2
    wide[...] = arrived[...].astype(F32)
    next_y = jnp.transpose(wide[pl.ds(3, width, stride=4), :])
    for side in range(2):
        both = wide[pl.ds(side * 4 + 2, deep, stride=8), :]
        for part in range(2):
            down = slice(part * deep, (part + 1) * deep)
            grouped[down, side * width : (side + 1) * width] = wide[
                pl.ds(side * 4 + part, deep, stride=8), :
            ]
            grouped[down, (2 + side) * width : (3 + side) * width] = (
                both if part == 0 else lane_roll(both, -8)
            )
    flat = jnp.transpose(grouped[...]).astype(BF16)
    mixed = lax.dot_general(flat, table[...], NN, preferred_element_type=F32)
    below = fine * rows
    real, imag = [], []
    for k in range(fine):
        cos = scale * turn_cos[k : k + 1, :]
        sin = scale * turn_sin[k : k + 1, :]
        at = k * rows
        both = jnp.concatenate([mixed[at : at + rows], mixed[below + at : below + at + 8]], 0)
        left, right = both[:, 0:width], both[:, width:]
        real.append(left * cos - right * sin)
        imag.append(right * cos + left * sin)
    even = [real[k] + real[fine - k] for k in range(1, half)]
    odd = [imag[k] - imag[fine - k] for k in range(1, half)]
    for c in range(half + 1):
        plain = weighted(
            [(1.0, real[0]), ((-1.0) ** c, real[half])]
            + [(cosine(c * k, fine), even[k - 1]) for k in range(1, half)]
        )
        cross = weighted([(sine(c * k, fine), odd[k - 1]) for k in range(1, half)])
        for index in sorted({c, (fine - c) % fine}):
            if cross is None:
                value = plain
            else:
                value = plain - cross if index == c else plain + cross
            span = slice(index * width, (index + 1) * width)
            push_x[:, span] = row_roll(value, -lead)[0:rows] * slope_x[:, span]
            push_y = value * jnp.concatenate(
                [slope_y[:, span], next_y[index * 8 : (index + 1) * 8]], 0
            )
            change = 8.0 * (row_roll(push_y, -1) - row_roll(push_y, -3)) - (
                push_y - row_roll(push_y, -4)
            )
            out[:, span] = change[0:rows] * (1.0 / 12.0)
    out[...] = out[...] - slope(push_x[...], lane_roll)


def whole(count):
    return [pl.BlockSpec(memory_space=pltpu.VMEM)] * count


def local(screens, image, vis_row, vis_block, vis_column, vis_real, vis_imag, vis_weight):
    rows, grid = image.shape
    slabs = lax.axis_size("slab")
    owned = grid // 2 // slabs
    slots = 3 * vis_row.shape[0] // slabs
    screen = screens.reshape(rows, grid)
    low, high = tables(rows, slabs, owned, grid)
    row_forward, row_back, coarse, coarse_back, inner, inner_back = low
    col_cos, col_sin, row_cos, row_sin = high
    width = slabs

    ring = [(i, (i + 1) % slabs) for i in range(slabs)]
    tail = jnp.concatenate([image[rows - halo :], screen[rows - halo :]], 0).astype(BF16)
    before = lax.ppermute(tail, "slab", ring)

    line = (1, vis_row.shape[0])
    limit = pltpu.CompilerParams(vmem_limit_bytes=12 * 2**20)
    place = pl.BlockSpec(memory_space=pltpu.VMEM)
    pay = pl.pallas_call(
        payload_kernel,
        out_shape=jax.ShapeDtypeStruct((slabs, width), F32),
        in_specs=whole(6),
        out_specs=place,
        scratch_shapes=[pltpu.VMEM((width, line[1]), F32)],
        compiler_params=limit,
        cost_estimate=pl.CostEstimate(flops=30_000_000, bytes_accessed=200_000, transcendentals=0),
        name="payload",
    )(
        vis_row.reshape(line), vis_block.reshape(line), vis_column.reshape(line),
        vis_real.reshape(line), vis_imag.reshape(line), vis_weight.reshape(line),
    )
    framed = rows + 8
    send, slope_x, slope_y = pl.pallas_call(
        spectrum_kernel,
        out_shape=[
            jax.ShapeDtypeStruct((4 * slabs, width), BF16),
            jax.ShapeDtypeStruct((rows, grid), F32),
            jax.ShapeDtypeStruct((rows, grid), F32),
        ],
        in_specs=whole(7),
        out_specs=whole(3),
        scratch_shapes=[
            pltpu.VMEM((framed, grid), F32),
            pltpu.VMEM((framed, grid), F32),
            pltpu.VMEM((2 * width, 2 * width), BF16),
            pltpu.VMEM((4 * slabs, width), F32),
            pltpu.VMEM((width, width), F32),
        ],
        compiler_params=limit,
        name="spectrum",
    )(screen, image, before, pay, row_forward, col_cos, col_sin)

    def exchange(block):
        return lax.all_to_all(
            block.reshape(slabs, 4, width), "slab", split_axis=0, concat_axis=0, tiled=True
        ).reshape(4 * slabs, width)

    scale = 1.0 / grid
    back = pl.pallas_call(
        lambda *refs: visibility_kernel(*refs, slots=slots, scale=scale),
        out_shape=jax.ShapeDtypeStruct((4 * slabs, width), BF16),
        in_specs=whole(7),
        out_specs=place,
        scratch_shapes=[
            pltpu.VMEM((4 * slabs, width), F32),
            pltpu.VMEM((2 * width, slots * width), BF16),
            pltpu.VMEM((2 * width, slots * width), BF16),
        ],
        compiler_params=limit,
        name="visibility",
    )(exchange(send), coarse, coarse_back, inner, inner_back, row_cos, row_sin)
    grad = pl.pallas_call(
        lambda *refs: gradient_kernel(*refs, scale=scale),
        out_shape=jax.ShapeDtypeStruct((rows, grid), F32),
        in_specs=whole(6),
        out_specs=place,
        scratch_shapes=[
            pltpu.VMEM((4 * slabs, width), F32),
            pltpu.VMEM((width, 4 * width), F32),
            pltpu.VMEM((rows, grid), F32),
        ],
        compiler_params=limit,
        name="gradient",
    )(exchange(back), slope_x, slope_y, row_back, col_cos, col_sin)
    return grad.reshape(1, rows, grid)


def solution(mesh):
    in_specs = (
        P(("chain", "vis"), "slab", None),
        P(("chain", "slab"), None),
        P("slab"),
        P("slab", None),
        P("slab"),
        P("slab"),
        P("slab"),
        P("slab"),
    )
    out_specs = P(("chain", "vis"), "slab", None)
    return jax.shard_map(local, mesh=mesh, in_specs=in_specs, out_specs=out_specs, check_vma=False)
```

time: 78.6 us -> 68.3 us (0.87)
  the two profiles are of different devices: /device:TPU:2 before, /device:TPU:8 now
where the time goes in v2:
time: 68.3 us; the launch traced here: 68 us
  blocking collectives  52 us (76%)
  waiting for transfers between devices  5.67 us (8%)
  Pallas kernels  3.69 us (5%)
  starting transfers between devices  3.62 us (5%)
  local copies, waits for them, and re-layouts  2.76 us (4%)
    all_to_all x2, blocking collectives, exchange(): lax.all_to_all(block.reshape(slabs, 4, width), 'slab', split_axis=0, conc...  52 us
    ppermute x1, waiting for transfers between devices, local(): before = lax.ppermute(tail, 'slab', ring)  5.67 us
    ppermute x1, starting transfers between devices, local(): before = lax.ppermute(tail, 'slab', ring)  3.62 us
  transfers between devices with their start and end apart: 1, of which 1 were waited for; matrix products, arithmetic and copies ran while one was open for 0% of the time, Pallas kernels for 1%

profile of v2, /device:TPU:8, one launch (start us, length us, event | category | flops | bytes accessed | tf_op | source)
XLA Modules:
  0.0 68.0 jit_solution(533159357177116879)
XLA Ops:
  0.0 0.9 %fusion = bf16[4,2048]{1,0:T(4,128)(2,1)S(1)} fusion(f32[1,16,2048]{2,1,0:T(8,128)} %param.18), kind=kLoop, calls=%fused_computation.3 | loop fusion | bytes 32768 | tf_op jit(solution)/shard_map/slice | solution.py:314
  0.9 0.9 %slice.20 = bf16[4,2048]{1,0:T(4,128)(2,1)S(1)} slice(f32[16,2048]{1,0:T(8,128)} %image.1), slice={[12:16], [0:2048]} | slice | bytes 32768 | tf_op jit(solution)/shard_map/slice | solution.py:314
  1.8 0.0 copy-start.11
  1.8 0.0 copy-start.12
  1.8 0.0 copy-start.13
  1.8 0.0 copy-start.14
  1.8 0.0 copy-start.15
  1.8 0.0 copy-start.16
  1.9 0.0 copy-start
  1.9 3.6 %collective-permute-start = (bf16[8,2048]{1,0:T(8,128)(2,1)S(1)}, bf16[8,2048]{1,0:T(8,128)(2,1)S(1)}, u32[]{:S(2)}, u32[]{:S(2)}) collective-permute-start(bf16[8,2048]{1,0:T(8,128)(2,1)S(1)} %pad_maximum_fusion), channel_id=1, source_target_pairs={{0,2},{2,4},{4,6},{6,8},{8,10},{10,12},{12,14},{14,16},{16,18},{18... | collective-permute-start | bytes 98312 | tf_op jit(solution)/shard_map/ppermute | solution.py:315
  5.5 0.0 copy-done.11
  5.5 0.0 copy-done.12
  5.5 0.0 copy-done.13
  5.6 0.0 copy-done.14
  5.6 0.0 copy-done.15
  5.6 0.0 copy-done.16
  5.6 0.0 copy-start.9
  5.6 0.0 copy-start.10
  5.6 0.4 payload.1.pay
  6.0 5.7 %collective-permute-done.before = bf16[8,2048]{1,0:T(8,128)(2,1)S(1)} collective-permute-done((bf16[8,2048]{1,0:T(8,128)(2,1)S(1)}, bf16[8,2048]{1,0:T(8,128)(2,1)S(1)}, u32[]{:S(2)}, u32[]{:S(2)}) %collective-permute-start) | collective-permute-done | bytes 32800 | tf_op jit(solution)/shard_map/ppermute | solution.py:315
  11.6 0.0 copy-done.1
  11.7 0.0 copy-done.9
  11.7 0.0 copy-done.10
  11.7 0.0 copy-start.2
  11.7 0.9 %copy-done.2 = f32[16,2048]{1,0:T(8,128)S(1)} copy-done((f32[16,2048]{1,0:T(8,128)S(1)}, f32[16,2048]{1,0:T(8,128)}, u32[]{:S(2)}) %copy-start.2) | copy-done | bytes 131096
  12.6 0.7 %spectrum.1 = (bf16[512,128]{1,0:T(8,128)(2,1)S(1)}, f32[16,2048]{1,0:T(8,128)S(1)}, f32[16,2048]{1,0:T(8,128)S(1)}) custom-call(f32[16,2048]{1,0:T(8,128)S(1)} %bitcast.17, f32[16,2048]{1,0:T(8,128)S(1)} %copy-done.2, bf16[8,2048]{1,0:T(8,128)(2,1)S(1)} %collective-permute-done.before, f32[128,128]{1,0:T(8,128)S(1)} %payload.1.pay, ...), custom_call_target="tpu_custom_call" | custom-call | tf_op jit(solution)/shard_map/spectrum/pallas_call | solution.py:334
  13.3 0.0 copy-start.3
  13.3 0.0 copy-start.4
  13.3 31.6 %all_to_all.10 = bf16[128,4,128]{2,1,0:T(4,128)(2,1)S(1)} all-to-all(bf16[128,4,128]{2,1,0:T(4,128)(2,1)S(1)} %bitcast.18), channel_id=1, replica_groups=mesh['chain'=2,'slab'=128,'vis'=2] {'slab'}, dimensions={0} | all-to-all | bytes 262144 | tf_op jit(solution)/shard_map/all_to_all | solution.py:355
  45.0 1.3 %visibility.1 = bf16[512,128]{1,0:T(8,128)(2,1)S(1)} custom-call(bf16[512,128]{1,0:T(8,128)(2,1)S(1)} %bitcast.14, bf16[256,256]{1,0:T(8,128)(2,1)S(1)} %copy-done.6, bf16[256,256]{1,0:T(8,128)(2,1)S(1)} %copy-done.5, bf16[256,256]{1,0:T(8,128)(2,1)S(1)} %copy-done.4, bf16[256,256]{1,0:T(8,128)(2,1)S(1)} %copy-done.3, f32[128,128]{1,0:T(8,128)S(1)} %copy-done.8, ...), custom_call_target="tpu_custom_call" | custom-call | tf_op jit(solution)/shard_map/visibility/pallas_call | solution.py:360
  46.3 20.4 %all_to_all.11 = bf16[128,4,128]{2,1,0:T(4,128)(2,1)S(1)} all-to-all(bf16[128,4,128]{2,1,0:T(4,128)(2,1)S(1)} %bitcast.15), channel_id=1, replica_groups=mesh['chain'=2,'slab'=128,'vis'=2] {'slab'}, dimensions={0} | all-to-all | bytes 262144 | tf_op jit(solution)/shard_map/all_to_all | solution.py:355
  66.7 1.3 %gradient.1 = f32[16,2048]{1,0:T(8,128)} custom-call(bf16[512,128]{1,0:T(8,128)(2,1)S(1)} %bitcast.16, f32[16,2048]{1,0:T(8,128)S(1)} %get-tuple-element.9.refs_1_, f32[16,2048]{1,0:T(8,128)S(1)} %get-tuple-element.10.refs_2_, bf16[128,256]{1,0:T(8,128)(2,1)S(1)} %copy-done, f32[16,128]{1,0:T(8,128)S(1)} %copy-done.10, f32[16,128]{1,0:T(8,128)S(1)} %copy-done.9), custom_call_target="tpu_custom_call" | custom-call | tf_op jit(solution)/shard_map/gradient/pallas_call | solution.py:373
  (13 shorter events, 0.0 us)
Async XLA Ops:
  0.0 11.6 %copy-start.1 = (f32[1,16,2048]{2,1,0:T(8,128)S(1)}, f32[1,16,2048]{2,1,0:T(8,128)}, u32[]{:S(2)}) copy-start(f32[1,16,2048]{2,1,0:T(8,128)} %param.18) | copy-start | bytes 393220
  1.8 3.7 %copy-start.11 = (s32[256]{0:T(256)S(1)}, s32[256]{0:T(256)}, u32[]{:S(2)}) copy-start(s32[256]{0:T(256)} %param.20) | copy-start | bytes 3076
  1.8 3.7 %copy-start.12 = (s32[256,1]{0,1:T(1,128)S(1)}, s32[256,1]{0,1:T(1,128)}, u32[]{:S(2)}) copy-start(s32[256,1]{0,1:T(1,128)} %param.21) | copy-start | bytes 3076
  1.8 3.7 %copy-start.13 = (s32[256]{0:T(256)S(1)}, s32[256]{0:T(256)}, u32[]{:S(2)}) copy-start(s32[256]{0:T(256)} %param.22) | copy-start | bytes 3076
  1.8 3.7 %copy-start.14 = (f32[256]{0:T(256)S(1)}, f32[256]{0:T(256)}, u32[]{:S(2)}) copy-start(f32[256]{0:T(256)} %param.23) | copy-start | bytes 3076
  1.8 3.7 %copy-start.15 = (f32[256]{0:T(256)S(1)}, f32[256]{0:T(256)}, u32[]{:S(2)}) copy-start(f32[256]{0:T(256)} %param.24) | copy-start | bytes 3076
  1.8 3.7 %copy-start.16 = (f32[256]{0:T(256)S(1)}, f32[256]{0:T(256)}, u32[]{:S(2)}) copy-start(f32[256]{0:T(256)} %param.25) | copy-start | bytes 3076
  1.9 9.8 %copy-start = (bf16[128,256]{1,0:T(8,128)(2,1)S(1)}, bf16[128,256]{1,0:T(8,128)(2,1)}, u32[]{:S(2)}) copy-start(bf16[128,256]{1,0:T(8,128)(2,1)} %constant.18.clone.table.refs_3_) | copy-start | bytes 196612
  1.9 9.7 %collective-permute-start = (bf16[8,2048]{1,0:T(8,128)(2,1)S(1)}, bf16[8,2048]{1,0:T(8,128)(2,1)S(1)}, u32[]{:S(2)}, u32[]{:S(2)}) collective-permute-start(bf16[8,2048]{1,0:T(8,128)(2,1)S(1)} %pad_maximum_fusion), channel_id=1, source_target_pairs={{0,2},{2,4},{4,6},{6,8},{8,10},{10,12},{12,14},{14,16},{16,18},{18... | collective-permute-start | bytes 98312 | tf_op jit(solution)/shard_map/ppermute | solution.py:315
  5.6 6.1 %copy-start.9 = (f32[16,128]{1,0:T(8,128)S(1)}, f32[16,128]{1,0:T(8,128)}, u32[]{:S(2)}) copy-start(f32[16,128]{1,0:T(8,128)} %constant.24.clone.turn_sin.refs_5_) | copy-start | bytes 24580
  5.6 6.1 %copy-start.10 = (f32[16,128]{1,0:T(8,128)S(1)}, f32[16,128]{1,0:T(8,128)}, u32[]{:S(2)}) copy-start(f32[16,128]{1,0:T(8,128)} %constant.23.clone.turn_cos.refs_4_) | copy-start | bytes 24580
  11.7 0.9 %copy-start.2 = (f32[16,2048]{1,0:T(8,128)S(1)}, f32[16,2048]{1,0:T(8,128)}, u32[]{:S(2)}) copy-start(f32[16,2048]{1,0:T(8,128)} %image.1) | copy-start | bytes 393220
  12.6 32.4 %copy-start.5 = (bf16[256,256]{1,0:T(8,128)(2,1)S(1)}, bf16[256,256]{1,0:T(8,128)(2,1)}, u32[]{:S(2)}) copy-start(bf16[256,256]{1,0:T(8,128)(2,1)} %constant.20.clone.refs_2_) | copy-start | bytes 393220
  12.6 32.4 %copy-start.6 = (bf16[256,256]{1,0:T(8,128)(2,1)S(1)}, bf16[256,256]{1,0:T(8,128)(2,1)}, u32[]{:S(2)}) copy-start(bf16[256,256]{1,0:T(8,128)(2,1)} %constant.19.clone.refs_1_) | copy-start | bytes 393220
  12.6 32.4 %copy-start.7 = (f32[128,128]{1,0:T(8,128)S(1)}, f32[128,128]{1,0:T(8,128)}, u32[]{:S(2)}) copy-start(f32[128,128]{1,0:T(8,128)} %constant.26.clone.refs_6_) | copy-start | bytes 196612
  12.6 32.4 %copy-start.8 = (f32[128,128]{1,0:T(8,128)S(1)}, f32[128,128]{1,0:T(8,128)}, u32[]{:S(2)}) copy-start(f32[128,128]{1,0:T(8,128)} %constant.25.clone.refs_5_) | copy-start | bytes 196612
  13.3 31.7 %copy-start.3 = (bf16[256,256]{1,0:T(8,128)(2,1)S(1)}, bf16[256,256]{1,0:T(8,128)(2,1)}, u32[]{:S(2)}) copy-start(bf16[256,256]{1,0:T(8,128)(2,1)} %constant.22.clone.refs_4_) | copy-start | bytes 393220
  13.3 31.7 %copy-start.4 = (bf16[256,256]{1,0:T(8,128)(2,1)S(1)}, bf16[256,256]{1,0:T(8,128)(2,1)}, u32[]{:S(2)}) copy-start(bf16[256,256]{1,0:T(8,128)(2,1)} %constant.21.clone.refs_3_) | copy-start | bytes 393220

commit v3 on v2

--- a/solution.py
+++ b/solution.py
@@ -110,6 +110,26 @@
             term = factor * value
         total = term if total is None else total + term
     return total
+
+
+def tail_kernel(image, screen, image_kept, screen_kept, tail, done):
+    rows = image.shape[0]
+    middle = rows // 2
+    moves = []
+    for first, last in ((middle, rows), (0, middle)):
+        for source, target in ((image, image_kept), (screen, screen_kept)):
+            move = pltpu.make_async_copy(
+                source.at[first:last, :], target.at[first:last, :], done.at[len(moves)]
+            )
+            move.start()
+            moves.append(move)
+    moves[0].wait()
+    moves[1].wait()
+    tail[...] = jnp.concatenate(
+        [image_kept[rows - halo :, :], screen_kept[rows - halo :, :]], 0
+    ).astype(BF16)
+    moves[2].wait()
+    moves[3].wait()
 
 
 def spectrum_kernel(
@@ -311,11 +331,20 @@
     width = slabs
 
     ring = [(i, (i + 1) % slabs) for i in range(slabs)]
-    tail = jnp.concatenate([image[rows - halo :], screen[rows - halo :]], 0).astype(BF16)
+    limit = pltpu.CompilerParams(vmem_limit_bytes=12 * 2**20)
+    field = jax.ShapeDtypeStruct((rows, grid), F32)
+    image, screen, tail = pl.pallas_call(
+        tail_kernel,
+        out_shape=[field, field, jax.ShapeDtypeStruct((2 * halo, grid), BF16)],
+        in_specs=[pl.BlockSpec(memory_space=pltpu.HBM)] * 2,
+        out_specs=whole(3),
+        scratch_shapes=[pltpu.SemaphoreType.DMA((4,))],
+        compiler_params=limit,
+        name="tail",
+    )(*(pltpu.with_memory_space_constraint(part, pltpu.HBM) for part in (image, screen)))
     before = lax.ppermute(tail, "slab", ring)
 
     line = (1, vis_row.shape[0])
-    limit = pltpu.CompilerParams(vmem_limit_bytes=12 * 2**20)
     place = pl.BlockSpec(memory_space=pltpu.VMEM)
     pay = pl.pallas_call(
         payload_kernel,

time: 68.3 us -> 66.6 us (0.975)
  local copies, waits for them, and re-layouts: 2.76 us -> 0.09 us
  Pallas kernels: 3.69 us -> 4.72 us
    slice x2 -> x0, local copies, waits for them, and re-layouts: 1.77 us -> none  [the longest x1 0.92 us: local(): screen[rows - halo:]]
    pallas_call x0 -> x1, Pallas kernels: none -> 1.02 us  [local(): pl.pallas_call(tail_kernel, out_shape=[field, field, jax.ShapeDtypeStruct...]
    unnamed x34 -> x30, local copies, waits for them, and re-layouts: 0.99 us -> 0.09 us
where the time goes in v3:
time: 66.6 us; the launch traced here: 66.3 us
  blocking collectives  52 us (78%)
  waiting for transfers between devices  5.67 us (9%)
  Pallas kernels  4.72 us (7%)
  starting transfers between devices  3.62 us (5%)
    all_to_all x2, blocking collectives, exchange(): lax.all_to_all(block.reshape(slabs, 4, width), 'slab', split_axis=0, conc...  52 us
    ppermute x1, waiting for transfers between devices, local(): before = lax.ppermute(tail, 'slab', ring)  5.67 us
    ppermute x1, starting transfers between devices, local(): before = lax.ppermute(tail, 'slab', ring)  3.62 us
    pallas_call x1, Pallas kernels, local(): pl.pallas_call(lambda *refs: visibility_kernel(*refs, slots=slots, scale=...  1.34 us
  transfers between devices with their start and end apart: 1, of which 1 were waited for; matrix products, arithmetic and copies ran while one was open for 0% of the time, Pallas kernels for 1%

profile of v3, /device:TPU:8, one launch (start us, length us, event | category | flops | bytes accessed | tf_op | source)
XLA Modules:
  0.0 66.3 jit_solution(1834236351951835853)
XLA Ops:
  0.0 0.0 copy-start.12
  0.0 0.0 copy-start.13
  0.0 0.0 copy-start.14
  0.0 1.0 %tail.1 = (f32[16,2048]{1,0:T(8,128)S(1)}, f32[16,2048]{1,0:T(8,128)S(1)}, bf16[8,2048]{1,0:T(8,128)(2,1)S(1)}) custom-call(f32[16,2048]{1,0:T(8,128)} %image.1, f32[16,2048]{1,0:T(8,128)} %bitcast.22), custom_call_target="tpu_custom_call" | custom-call | tf_op jit(solution)/shard_map/tail/pallas_call | solution.py:336
  1.1 0.0 copy-start
  1.1 3.6 %collective-permute-start = (bf16[8,2048]{1,0:T(8,128)(2,1)S(1)}, bf16[8,2048]{1,0:T(8,128)(2,1)S(1)}, u32[]{:S(2)}, u32[]{:S(2)}) collective-permute-start(bf16[8,2048]{1,0:T(8,128)(2,1)S(1)} %get-tuple-element.13), channel_id=1, source_target_pairs={{0,2},{2,4},{4,6},{6,8},{8,10},{10,12},{12,14},{14,16},{16,18},{18... | collective-permute-start | bytes 98312 | tf_op jit(solution)/shard_map/ppermute | solution.py:345
  4.7 0.0 copy-done.9
  4.7 0.0 copy-done.10
  4.7 0.0 copy-done.11
  4.7 0.0 copy-done.12
  4.7 0.0 copy-done.13
  4.8 0.0 copy-done.14
  4.8 0.0 copy-start.7
  4.8 0.0 copy-start.8
  4.8 0.4 payload.1.pay
  5.2 5.7 %collective-permute-done.before = bf16[8,2048]{1,0:T(8,128)(2,1)S(1)} collective-permute-done((bf16[8,2048]{1,0:T(8,128)(2,1)S(1)}, bf16[8,2048]{1,0:T(8,128)(2,1)S(1)}, u32[]{:S(2)}, u32[]{:S(2)}) %collective-permute-start) | collective-permute-done | bytes 32800 | tf_op jit(solution)/shard_map/ppermute | solution.py:345
  10.8 0.0 copy-done
  10.8 0.0 copy-done.7
  10.8 0.0 copy-done.8
  10.8 0.0 copy-start.3
  10.9 0.0 copy-start.4
  10.9 0.0 copy-start.5
  10.9 0.0 copy-start.6
  10.9 0.7 %spectrum.1 = (bf16[512,128]{1,0:T(8,128)(2,1)S(1)}, f32[16,2048]{1,0:T(8,128)S(1)}, f32[16,2048]{1,0:T(8,128)S(1)}) custom-call(f32[16,2048]{1,0:T(8,128)S(1)} %get-tuple-element.11.screen, f32[16,2048]{1,0:T(8,128)S(1)} %get-tuple-element.12.image, bf16[8,2048]{1,0:T(8,128)(2,1)S(1)} %collective-permute-done.before, f32[128,128]{1,0:T(8,128)S(1)} %payload.1.pay, ...), custom_call_target="tpu_custom_call" | custom-call | tf_op jit(solution)/shard_map/spectrum/pallas_call | solution.py:363
  11.6 0.0 copy-start.1
  11.6 0.0 copy-start.2
  11.6 31.6 %all_to_all.10 = bf16[128,4,128]{2,1,0:T(4,128)(2,1)S(1)} all-to-all(bf16[128,4,128]{2,1,0:T(4,128)(2,1)S(1)} %bitcast.15), channel_id=1, replica_groups=mesh['chain'=2,'slab'=128,'vis'=2] {'slab'}, dimensions={0} | all-to-all | bytes 262144 | tf_op jit(solution)/shard_map/all_to_all | solution.py:384
  43.2 0.0 copy-done.3
  43.2 0.0 copy-done.4
  43.3 1.3 %visibility.1 = bf16[512,128]{1,0:T(8,128)(2,1)S(1)} custom-call(bf16[512,128]{1,0:T(8,128)(2,1)S(1)} %bitcast.12, bf16[256,256]{1,0:T(8,128)(2,1)S(1)} %copy-done.4, bf16[256,256]{1,0:T(8,128)(2,1)S(1)} %copy-done.3, bf16[256,256]{1,0:T(8,128)(2,1)S(1)} %copy-done.2, bf16[256,256]{1,0:T(8,128)(2,1)S(1)} %copy-done.1, f32[128,128]{1,0:T(8,128)S(1)} %copy-done.6, ...), custom_call_target="tpu_custom_call" | custom-call | tf_op jit(solution)/shard_map/visibility/pallas_call | solution.py:389
  44.6 20.4 %all_to_all.11 = bf16[128,4,128]{2,1,0:T(4,128)(2,1)S(1)} all-to-all(bf16[128,4,128]{2,1,0:T(4,128)(2,1)S(1)} %bitcast.13), channel_id=1, replica_groups=mesh['chain'=2,'slab'=128,'vis'=2] {'slab'}, dimensions={0} | all-to-all | bytes 262144 | tf_op jit(solution)/shard_map/all_to_all | solution.py:384
  65.0 1.3 %gradient.1 = f32[16,2048]{1,0:T(8,128)} custom-call(bf16[512,128]{1,0:T(8,128)(2,1)S(1)} %bitcast.14, f32[16,2048]{1,0:T(8,128)S(1)} %get-tuple-element.15.refs_1_, f32[16,2048]{1,0:T(8,128)S(1)} %get-tuple-element.16.refs_2_, bf16[128,256]{1,0:T(8,128)(2,1)S(1)} %copy-done, f32[16,128]{1,0:T(8,128)S(1)} %copy-done.8, f32[16,128]{1,0:T(8,128)S(1)} %copy-done.7), custom_call_target="tpu_custom_call" | custom-call | tf_op jit(solution)/shard_map/gradient/pallas_call | solution.py:402
  (7 shorter events, 0.0 us)
Async XLA Ops:
  0.0 4.7 %copy-start.9 = (s32[256]{0:T(256)S(1)}, s32[256]{0:T(256)}, u32[]{:S(2)}) copy-start(s32[256]{0:T(256)} %param.20) | copy-start | bytes 3076
  0.0 4.7 %copy-start.10 = (s32[256,1]{0,1:T(1,128)S(1)}, s32[256,1]{0,1:T(1,128)}, u32[]{:S(2)}) copy-start(s32[256,1]{0,1:T(1,128)} %param.21) | copy-start | bytes 3076
  0.0 4.7 %copy-start.11 = (s32[256]{0:T(256)S(1)}, s32[256]{0:T(256)}, u32[]{:S(2)}) copy-start(s32[256]{0:T(256)} %param.22) | copy-start | bytes 3076
  0.0 4.7 %copy-start.12 = (f32[256]{0:T(256)S(1)}, f32[256]{0:T(256)}, u32[]{:S(2)}) copy-start(f32[256]{0:T(256)} %param.23) | copy-start | bytes 3076
  0.0 4.7 %copy-start.13 = (f32[256]{0:T(256)S(1)}, f32[256]{0:T(256)}, u32[]{:S(2)}) copy-start(f32[256]{0:T(256)} %param.24) | copy-start | bytes 3076
  0.0 4.7 %copy-start.14 = (f32[256]{0:T(256)S(1)}, f32[256]{0:T(256)}, u32[]{:S(2)}) copy-start(f32[256]{0:T(256)} %param.25) | copy-start | bytes 3076
  1.1 9.8 %copy-start = (bf16[128,256]{1,0:T(8,128)(2,1)S(1)}, bf16[128,256]{1,0:T(8,128)(2,1)}, u32[]{:S(2)}) copy-start(bf16[128,256]{1,0:T(8,128)(2,1)} %constant.18.clone.table.refs_3_) | copy-start | bytes 196612
  1.1 9.7 %collective-permute-start = (bf16[8,2048]{1,0:T(8,128)(2,1)S(1)}, bf16[8,2048]{1,0:T(8,128)(2,1)S(1)}, u32[]{:S(2)}, u32[]{:S(2)}) collective-permute-start(bf16[8,2048]{1,0:T(8,128)(2,1)S(1)} %get-tuple-element.13), channel_id=1, source_target_pairs={{0,2},{2,4},{4,6},{6,8},{8,10},{10,12},{12,14},{14,16},{16,18},{18... | collective-permute-start | bytes 98312 | tf_op jit(solution)/shard_map/ppermute | solution.py:345
  4.8 6.1 %copy-start.7 = (f32[16,128]{1,0:T(8,128)S(1)}, f32[16,128]{1,0:T(8,128)}, u32[]{:S(2)}) copy-start(f32[16,128]{1,0:T(8,128)} %constant.24.clone.turn_sin.refs_5_) | copy-start | bytes 24580
  4.8 6.1 %copy-start.8 = (f32[16,128]{1,0:T(8,128)S(1)}, f32[16,128]{1,0:T(8,128)}, u32[]{:S(2)}) copy-start(f32[16,128]{1,0:T(8,128)} %constant.23.clone.turn_cos.refs_4_) | copy-start | bytes 24580
  10.8 32.4 %copy-start.3 = (bf16[256,256]{1,0:T(8,128)(2,1)S(1)}, bf16[256,256]{1,0:T(8,128)(2,1)}, u32[]{:S(2)}) copy-start(bf16[256,256]{1,0:T(8,128)(2,1)} %constant.20.clone.refs_2_) | copy-start | bytes 393220
  10.9 32.4 %copy-start.4 = (bf16[256,256]{1,0:T(8,128)(2,1)S(1)}, bf16[256,256]{1,0:T(8,128)(2,1)}, u32[]{:S(2)}) copy-start(bf16[256,256]{1,0:T(8,128)(2,1)} %constant.19.clone.refs_1_) | copy-start | bytes 393220
  10.9 32.4 %copy-start.5 = (f32[128,128]{1,0:T(8,128)S(1)}, f32[128,128]{1,0:T(8,128)}, u32[]{:S(2)}) copy-start(f32[128,128]{1,0:T(8,128)} %constant.26.clone.refs_6_) | copy-start | bytes 196612
  10.9 32.4 %copy-start.6 = (f32[128,128]{1,0:T(8,128)S(1)}, f32[128,128]{1,0:T(8,128)}, u32[]{:S(2)}) copy-start(f32[128,128]{1,0:T(8,128)} %constant.25.clone.refs_5_) | copy-start | bytes 196612
  11.6 31.7 %copy-start.1 = (bf16[256,256]{1,0:T(8,128)(2,1)S(1)}, bf16[256,256]{1,0:T(8,128)(2,1)}, u32[]{:S(2)}) copy-start(bf16[256,256]{1,0:T(8,128)(2,1)} %constant.22.clone.refs_4_) | copy-start | bytes 393220
  11.6 31.7 %copy-start.2 = (bf16[256,256]{1,0:T(8,128)(2,1)S(1)}, bf16[256,256]{1,0:T(8,128)(2,1)}, u32[]{:S(2)}) copy-start(bf16[256,256]{1,0:T(8,128)(2,1)} %constant.21.clone.refs_3_) | copy-start | bytes 393220

commit v4 on v2

--- a/solution.py
+++ b/solution.py
@@ -42,7 +42,18 @@
     return [jnp.asarray(t, BF16) for t in low], [jnp.asarray(t, F32) for t in high]
 
 
-def payload_kernel(row, block, column, real, imag, weight, out, wide):
+def payload_kernel(
+    image, screen, row, block, column, real, imag, weight,
+    out, image_kept, screen_kept, base, slope_x, wide, done,
+):
+    moves = [
+        pltpu.make_async_copy(source, target, done.at[index])
+        for index, (source, target) in enumerate(
+            ((image, image_kept), (screen, screen_kept))
+        )
+    ]
+    for move in moves:
+        move.start()
     vis_count = row.shape[1]
     slabs = out.shape[0]
     hot = (
@@ -75,6 +86,12 @@
     out[...] = lax.dot_general(
         hot_low, wide[...].astype(BF16), NT, preferred_element_type=F32
     )
+    for move in moves:
+        move.wait()
+    own = image_kept[...]
+    own_x = slope(own, lane_roll)
+    slope_x[...] = own_x
+    base[...] = own + slope(screen_kept[...], lane_roll) * own_x
 
 
 def lane_roll(x, shift):
@@ -112,9 +129,31 @@
     return total
 
 
+def tail_kernel(image, screen, tail, kept, done):
+    rows, grid = image.shape
+    below, span = rows - 8, grid // 2
+    moves = []
+    for index, source in enumerate((image, screen)):
+        for side in range(2):
+            columns = slice(side * span, (side + 1) * span)
+            moves.append(
+                pltpu.make_async_copy(
+                    source.at[below:rows, columns],
+                    kept.at[index * 8 : (index + 1) * 8, columns],
+                    done.at[len(moves)],
+                )
+            )
+            moves[-1].start()
+    for move in moves:
+        move.wait()
+    tail[...] = jnp.concatenate(
+        [kept[8 - halo : 8, :], kept[16 - halo : 16, :]], 0
+    ).astype(BF16)
+
+
 def spectrum_kernel(
-    screen, image, before, pay, table, turn_cos, turn_sin,
-    out, slope_x, slope_y, frame, other, folded, packed, relayed,
+    screen, image, base, before, pay, table, turn_cos, turn_sin,
+    out, slope_y, frame, other, joint, folded, packed, relayed,
 ):
     rows, grid = image.shape
     fine, width = turn_cos.shape
@@ -126,16 +165,15 @@
         ref[lead : lead + rows, :] = own[...]
         ref[lead + rows : framed - lead, :] = jnp.zeros((framed - rows - 2 * lead, grid), F32)
         ref[framed - lead :, :] = part[: halo - lead]
-    field = frame[...]
-    image_x = slope(field, lane_roll)
-    image_y = slope(field, row_roll)
-    slope_x[...] = row_roll(image_x, -lead)[0:rows]
+    edge_x = slope(edge, lane_roll)
+    edge_base = edge[0:halo] + edge_x[halo:] * edge_x[0:halo]
+    joint[0:lead, :] = edge_base[halo - lead :]
+    joint[lead:, :] = base[0 : rows - lead, :]
+    image_y = slope(frame[...], row_roll)
     slope_y[...] = image_y[0:rows]
     for i in range(fine):
         relayed[i * 8 : (i + 1) * 8, :] = image_y[0:8, i * width : (i + 1) * width]
-    change = other[...]
-    change_x = slope(change[0:rows], lane_roll) * image_x[0:rows]
-    joined = field[0:rows] + change_x + (slope(change, row_roll) * image_y)[0:rows]
+    joined = joint[...] + (slope(other[...], row_roll) * image_y)[0:rows]
     tiles = [joined[:, i * width : (i + 1) * width] for i in range(fine)]
     half = fine // 2
     even = [tiles[j] + tiles[fine - j] for j in range(1, half)]
@@ -311,45 +349,58 @@
     width = slabs
 
     ring = [(i, (i + 1) % slabs) for i in range(slabs)]
-    tail = jnp.concatenate([image[rows - halo :], screen[rows - halo :]], 0).astype(BF16)
+    limit = pltpu.CompilerParams(vmem_limit_bytes=12 * 2**20)
+    field = jax.ShapeDtypeStruct((rows, grid), F32)
+    far = [pl.BlockSpec(memory_space=pltpu.HBM)] * 2
+    image, screen = (
+        pltpu.with_memory_space_constraint(part, pltpu.HBM) for part in (image, screen)
+    )
+    tail = pl.pallas_call(
+        tail_kernel,
+        out_shape=jax.ShapeDtypeStruct((2 * halo, grid), BF16),
+        in_specs=far,
+        out_specs=pl.BlockSpec(memory_space=pltpu.VMEM),
+        scratch_shapes=[pltpu.VMEM((16, grid), F32), pltpu.SemaphoreType.DMA((4,))],
+        compiler_params=limit,
+        name="tail",
+    )(image, screen)
     before = lax.ppermute(tail, "slab", ring)
 
     line = (1, vis_row.shape[0])
-    limit = pltpu.CompilerParams(vmem_limit_bytes=12 * 2**20)
     place = pl.BlockSpec(memory_space=pltpu.VMEM)
-    pay = pl.pallas_call(
+    pay, image, screen, base, slope_x = pl.pallas_call(
         payload_kernel,
-        out_shape=jax.ShapeDtypeStruct((slabs, width), F32),
-        in_specs=whole(6),
-        out_specs=place,
-        scratch_shapes=[pltpu.VMEM((width, line[1]), F32)],
+        out_shape=[jax.ShapeDtypeStruct((slabs, width), F32), field, field, field, field],
+        in_specs=far + whole(6),
+        out_specs=whole(5),
+        scratch_shapes=[pltpu.VMEM((width, line[1]), F32), pltpu.SemaphoreType.DMA((2,))],
         compiler_params=limit,
         cost_estimate=pl.CostEstimate(flops=30_000_000, bytes_accessed=200_000, transcendentals=0),
         name="payload",
     )(
-        vis_row.reshape(line), vis_block.reshape(line), vis_column.reshape(line),
+        image, screen, vis_row.reshape(line), vis_block.reshape(line), vis_column.reshape(line),
         vis_real.reshape(line), vis_imag.reshape(line), vis_weight.reshape(line),
     )
     framed = rows + 8
-    send, slope_x, slope_y = pl.pallas_call(
+    send, slope_y = pl.pallas_call(
         spectrum_kernel,
         out_shape=[
             jax.ShapeDtypeStruct((4 * slabs, width), BF16),
-            jax.ShapeDtypeStruct((rows, grid), F32),
-            jax.ShapeDtypeStruct((rows, grid), F32),
+            field,
         ],
-        in_specs=whole(7),
-        out_specs=whole(3),
+        in_specs=whole(8),
+        out_specs=whole(2),
         scratch_shapes=[
             pltpu.VMEM((framed, grid), F32),
             pltpu.VMEM((framed, grid), F32),
+            pltpu.VMEM((rows, grid), F32),
             pltpu.VMEM((2 * width, 2 * width), BF16),
             pltpu.VMEM((4 * slabs, width), F32),
             pltpu.VMEM((width, width), F32),
         ],
         compiler_params=limit,
         name="spectrum",
-    )(screen, image, before, pay, row_forward, col_cos, col_sin)
+    )(screen, image, base, before, pay, row_forward, col_cos, col_sin)
 
     def exchange(block):
         return lax.all_to_all(

time: 68.3 us -> 66.1 us (0.968)
  local copies, waits for them, and re-layouts: 2.76 us -> 0.76 us
  Pallas kernels: 3.69 us -> 5.37 us
  waiting for transfers between devices: 5.67 us -> 3.99 us
    pallas_call x1 -> x2, Pallas kernels: 0.36 us -> 2.21 us  [the longest x1 1.36 us: local(): pl.pallas_call(payload_kernel, out_shape=[jax.ShapeDtypeStruct((slabs, wi...]
    slice x2 -> x0, local copies, waits for them, and re-layouts: 1.77 us -> none  [the longest x1 0.92 us: local(): screen[rows - halo:]]
    ppermute x1, waiting for transfers between devices: 5.67 us -> 3.99 us  [local(): before = lax.ppermute(tail, 'slab', ring)]
  transfers between devices with their start and end apart: 1 -> 1, of which waited for: 1 -> 1; matrix products, arithmetic and copies ran while one was open for 0% -> 0% of each run, Pallas kernels for 1% -> 2%
where the time goes in v4:
time: 66.1 us; the launch traced here: 65.8 us
  blocking collectives  52 us (79%)
  Pallas kernels  5.37 us (8%)
  waiting for transfers between devices  3.99 us (6%)
  starting transfers between devices  3.48 us (5%)
  local copies, waits for them, and re-layouts  0.76 us (1%)
    all_to_all x2, blocking collectives, exchange(): lax.all_to_all(block.reshape(slabs, 4, width), 'slab', split_axis=0, conc...  52 us
    ppermute x1, waiting for transfers between devices, local(): before = lax.ppermute(tail, 'slab', ring)  3.99 us
    ppermute x1, starting transfers between devices, local(): before = lax.ppermute(tail, 'slab', ring)  3.48 us
    pallas_call x1, Pallas kernels, local(): pl.pallas_call(payload_kernel, out_shape=[jax.ShapeDtypeStruct((slabs, wi...  1.36 us
    pallas_call x1, Pallas kernels, local(): pl.pallas_call(lambda *refs: visibility_kernel(*refs, slots=slots, scale=...  1.34 us
  transfers between devices with their start and end apart: 1, of which 1 were waited for; matrix products, arithmetic and copies ran while one was open for 0% of the time, Pallas kernels for 2%

profile of v4, /device:TPU:8, one launch (start us, length us, event | category | flops | bytes accessed | tf_op | source)
XLA Modules:
  0.0 65.8 jit_solution(5187043207085579729)
XLA Ops:
  0.0 0.9 %tail.1 = bf16[8,2048]{1,0:T(8,128)(2,1)S(1)} custom-call(f32[16,2048]{1,0:T(8,128)} %image.3, f32[16,2048]{1,0:T(8,128)} %bitcast.22), custom_call_target="tpu_custom_call" | custom-call | tf_op jit(solution)/shard_map/tail/pallas_call | solution.py:358
  0.9 3.5 %collective-permute-start = (bf16[8,2048]{1,0:T(8,128)(2,1)S(1)}, bf16[8,2048]{1,0:T(8,128)(2,1)S(1)}, u32[]{:S(2)}, u32[]{:S(2)}) collective-permute-start(bf16[8,2048]{1,0:T(8,128)(2,1)S(1)} %tail.1), channel_id=1, source_target_pairs={{0,2},{2,4},{4,6},{6,8},{8,10},{10,12},{12,14},{14,16},{16,18},{18... | collective-permute-start | bytes 98312 | tf_op jit(solution)/shard_map/ppermute | solution.py:367
  4.4 0.0 copy-start.14
  4.4 0.0 copy-start.10
  4.4 0.0 copy-start.11
  4.4 0.0 copy-start.12
  4.4 0.0 copy-start.13
  4.4 0.0 copy-start.9
  4.4 0.6 copy-done.14
  5.0 0.0 copy-done.10
  5.0 0.0 copy-done.11
  5.1 0.0 copy-done.12
  5.1 0.0 copy-done.13
  5.1 0.0 copy-done.9
  5.1 1.4 %payload.1 = (f32[128,128]{1,0:T(8,128)S(1)}, f32[16,2048]{1,0:T(8,128)S(1)}, f32[16,2048]{1,0:T(8,128)S(1)}, f32[16,2048]{1,0:T(8,128)S(1)}, f32[16,2048]{1,0:T(8,128)S(1)}) custom-call(f32[16,2048]{1,0:T(8,128)} %image.3, f32[16,2048]{1,0:T(8,128)} %bitcast.23, s32[1,256]{1,0:T(1,128)S(1)} %bitcast.16, s32[1,256]{1,0:T(1,128)S(1)} %bitcast.17, ...), custom_call_target="tpu_custom_call" | custom-call | flops 30000000 | bytes 200000 | tf_op jit(solution)/shard_map/payload/pallas_call | solution.py:371
  6.5 4.0 %collective-permute-done.before = bf16[8,2048]{1,0:T(8,128)(2,1)S(1)} collective-permute-done((bf16[8,2048]{1,0:T(8,128)(2,1)S(1)}, bf16[8,2048]{1,0:T(8,128)(2,1)S(1)}, u32[]{:S(2)}, u32[]{:S(2)}) %collective-permute-start) | collective-permute-done | bytes 32800 | tf_op jit(solution)/shard_map/ppermute | solution.py:367
  10.5 0.0 copy-done
  10.5 0.0 copy-done.7
  10.5 0.0 copy-done.8
  10.5 0.0 copy-start.3
  10.5 0.0 copy-start.4
  10.5 0.0 copy-start.5
  10.5 0.0 copy-start.6
  10.5 0.5 spectrum.1
  11.1 0.0 copy-start.1
  11.1 0.0 copy-start.2
  11.1 31.6 %all_to_all.10 = bf16[128,4,128]{2,1,0:T(4,128)(2,1)S(1)} all-to-all(bf16[128,4,128]{2,1,0:T(4,128)(2,1)S(1)} %bitcast.15), channel_id=1, replica_groups=mesh['chain'=2,'slab'=128,'vis'=2] {'slab'}, dimensions={0} | all-to-all | bytes 262144 | tf_op jit(solution)/shard_map/all_to_all | solution.py:406
  42.7 0.0 copy-done.3
  42.7 0.0 copy-done.4
  42.8 1.3 %visibility.1 = bf16[512,128]{1,0:T(8,128)(2,1)S(1)} custom-call(bf16[512,128]{1,0:T(8,128)(2,1)S(1)} %bitcast.13, bf16[256,256]{1,0:T(8,128)(2,1)S(1)} %copy-done.4, bf16[256,256]{1,0:T(8,128)(2,1)S(1)} %copy-done.3, bf16[256,256]{1,0:T(8,128)(2,1)S(1)} %copy-done.2, bf16[256,256]{1,0:T(8,128)(2,1)S(1)} %copy-done.1, f32[128,128]{1,0:T(8,128)S(1)} %copy-done.6, ...), custom_call_target="tpu_custom_call" | custom-call | tf_op jit(solution)/shard_map/visibility/pallas_call | solution.py:411
  44.1 20.4 %all_to_all.11 = bf16[128,4,128]{2,1,0:T(4,128)(2,1)S(1)} all-to-all(bf16[128,4,128]{2,1,0:T(4,128)(2,1)S(1)} %bitcast.14), channel_id=1, replica_groups=mesh['chain'=2,'slab'=128,'vis'=2] {'slab'}, dimensions={0} | all-to-all | bytes 262144 | tf_op jit(solution)/shard_map/all_to_all | solution.py:406
  64.5 1.3 %gradient.1 = f32[16,2048]{1,0:T(8,128)} custom-call(bf16[512,128]{1,0:T(8,128)(2,1)S(1)} %bitcast.12, f32[16,2048]{1,0:T(8,128)S(1)} %get-tuple-element.17.refs_1_, f32[16,2048]{1,0:T(8,128)S(1)} %get-tuple-element.18.refs_2_, bf16[128,256]{1,0:T(8,128)(2,1)S(1)} %copy-done, f32[16,128]{1,0:T(8,128)S(1)} %copy-done.8, f32[16,128]{1,0:T(8,128)S(1)} %copy-done.7), custom_call_target="tpu_custom_call" | custom-call | tf_op jit(solution)/shard_map/gradient/pallas_call | solution.py:424
  (7 shorter events, 0.0 us)
Async XLA Ops:
  0.9 9.6 %collective-permute-start = (bf16[8,2048]{1,0:T(8,128)(2,1)S(1)}, bf16[8,2048]{1,0:T(8,128)(2,1)S(1)}, u32[]{:S(2)}, u32[]{:S(2)}) collective-permute-start(bf16[8,2048]{1,0:T(8,128)(2,1)S(1)} %tail.1), channel_id=1, source_target_pairs={{0,2},{2,4},{4,6},{6,8},{8,10},{10,12},{12,14},{14,16},{16,18},{18... | collective-permute-start | bytes 98312 | tf_op jit(solution)/shard_map/ppermute | solution.py:367
  4.4 0.7 %copy-start.14 = (f32[256]{0:T(256)S(1)}, f32[256]{0:T(256)}, u32[]{:S(2)}) copy-start(f32[256]{0:T(256)} %param.25) | copy-start | bytes 3076
  4.4 0.7 %copy-start.10 = (s32[256,1]{0,1:T(1,128)S(1)}, s32[256,1]{0,1:T(1,128)}, u32[]{:S(2)}) copy-start(s32[256,1]{0,1:T(1,128)} %param.21) | copy-start | bytes 3076
  4.4 0.7 %copy-start.11 = (s32[256]{0:T(256)S(1)}, s32[256]{0:T(256)}, u32[]{:S(2)}) copy-start(s32[256]{0:T(256)} %param.22) | copy-start | bytes 3076
  4.4 0.7 %copy-start.12 = (f32[256]{0:T(256)S(1)}, f32[256]{0:T(256)}, u32[]{:S(2)}) copy-start(f32[256]{0:T(256)} %param.23) | copy-start | bytes 3076
  4.4 0.7 %copy-start.13 = (f32[256]{0:T(256)S(1)}, f32[256]{0:T(256)}, u32[]{:S(2)}) copy-start(f32[256]{0:T(256)} %param.24) | copy-start | bytes 3076
  4.4 0.7 %copy-start.9 = (s32[256]{0:T(256)S(1)}, s32[256]{0:T(256)}, u32[]{:S(2)}) copy-start(s32[256]{0:T(256)} %param.20) | copy-start | bytes 3076
  5.1 5.4 %copy-start = (bf16[128,256]{1,0:T(8,128)(2,1)S(1)}, bf16[128,256]{1,0:T(8,128)(2,1)}, u32[]{:S(2)}) copy-start(bf16[128,256]{1,0:T(8,128)(2,1)} %constant.18.clone.table.refs_3_) | copy-start | bytes 196612
  5.1 5.4 %copy-start.7 = (f32[16,128]{1,0:T(8,128)S(1)}, f32[16,128]{1,0:T(8,128)}, u32[]{:S(2)}) copy-start(f32[16,128]{1,0:T(8,128)} %constant.24.clone.turn_sin.refs_5_) | copy-start | bytes 24580
  5.1 5.4 %copy-start.8 = (f32[16,128]{1,0:T(8,128)S(1)}, f32[16,128]{1,0:T(8,128)}, u32[]{:S(2)}) copy-start(f32[16,128]{1,0:T(8,128)} %constant.23.clone.turn_cos.refs_4_) | copy-start | bytes 24580
  10.5 32.2 %copy-start.3 = (bf16[256,256]{1,0:T(8,128)(2,1)S(1)}, bf16[256,256]{1,0:T(8,128)(2,1)}, u32[]{:S(2)}) copy-start(bf16[256,256]{1,0:T(8,128)(2,1)} %constant.20.clone.refs_2_) | copy-start | bytes 393220
  10.5 32.2 %copy-start.4 = (bf16[256,256]{1,0:T(8,128)(2,1)S(1)}, bf16[256,256]{1,0:T(8,128)(2,1)}, u32[]{:S(2)}) copy-start(bf16[256,256]{1,0:T(8,128)(2,1)} %constant.19.clone.refs_1_) | copy-start | bytes 393220
  10.5 32.2 %copy-start.5 = (f32[128,128]{1,0:T(8,128)S(1)}, f32[128,128]{1,0:T(8,128)}, u32[]{:S(2)}) copy-start(f32[128,128]{1,0:T(8,128)} %constant.26.clone.refs_6_) | copy-start | bytes 196612
  10.5 32.2 %copy-start.6 = (f32[128,128]{1,0:T(8,128)S(1)}, f32[128,128]{1,0:T(8,128)}, u32[]{:S(2)}) copy-start(f32[128,128]{1,0:T(8,128)} %constant.25.clone.refs_5_) | copy-start | bytes 196612
  11.1 31.7 %copy-start.1 = (bf16[256,256]{1,0:T(8,128)(2,1)S(1)}, bf16[256,256]{1,0:T(8,128)(2,1)}, u32[]{:S(2)}) copy-start(bf16[256,256]{1,0:T(8,128)(2,1)} %constant.22.clone.refs_4_) | copy-start | bytes 393220
  11.1 31.7 %copy-start.2 = (bf16[256,256]{1,0:T(8,128)(2,1)S(1)}, bf16[256,256]{1,0:T(8,128)(2,1)}, u32[]{:S(2)}) copy-start(bf16[256,256]{1,0:T(8,128)(2,1)} %constant.21.clone.refs_3_) | copy-start | bytes 393220

commit v5 on v4

--- a/solution.py
+++ b/solution.py
@@ -278,7 +278,7 @@
 
 def gradient_kernel(
     arrived, slope_x, slope_y, table, turn_cos, turn_sin,
-    out, wide, grouped, push_x, *, scale,
+    out, wide, grouped, result, done, *, scale,
 ):
     rows, grid = slope_x.shape
     fine, width = turn_cos.shape
@@ -310,6 +310,8 @@
         imag.append(right * cos + left * sin)
     even = [real[k] + real[fine - k] for k in range(1, half)]
     odd = [imag[k] - imag[fine - k] for k in range(1, half)]
+    lane = lax.broadcasted_iota(jnp.int32, (rows, width), 1)
+    parts, turned, finished, moves = {}, {}, set(), {}
     for c in range(half + 1):
         plain = weighted(
             [(1.0, real[0]), ((-1.0) ** c, real[half])]
@@ -322,15 +324,42 @@
             else:
                 value = plain - cross if index == c else plain + cross
             span = slice(index * width, (index + 1) * width)
-            push_x[:, span] = row_roll(value, -lead)[0:rows] * slope_x[:, span]
+            push_x = row_roll(value, -lead)[0:rows] * slope_x[:, span]
+            turned[index] = {step: lane_roll(push_x, -step) for step in (-2, -1, 1, 2)}
             push_y = value * jnp.concatenate(
                 [slope_y[:, span], next_y[index * 8 : (index + 1) * 8]], 0
             )
             change = 8.0 * (row_roll(push_y, -1) - row_roll(push_y, -3)) - (
                 push_y - row_roll(push_y, -4)
             )
-            out[:, span] = change[0:rows] * (1.0 / 12.0)
-    out[...] = out[...] - slope(push_x[...], lane_roll)
+            parts[index] = change[0:rows] * (1.0 / 12.0)
+        for index in range(fine):
+            left, right = (index - 1) % fine, (index + 1) % fine
+            if index in finished or not {left, index, right} <= parts.keys():
+                continue
+            near = {
+                step: jnp.where(
+                    lane < width - step if step > 0 else lane >= -step,
+                    turned[index][step],
+                    turned[right if step > 0 else left][step],
+                )
+                for step in (-2, -1, 1, 2)
+            }
+            change = 8.0 * (near[1] - near[-1]) - (near[2] - near[-2])
+            result[:, index * width : (index + 1) * width] = (
+                parts[index] - change * (1.0 / 12.0)
+            )
+            finished.add(index)
+        for pair in range(half):
+            if pair in moves or not {2 * pair, 2 * pair + 1} <= finished:
+                continue
+            span = slice(2 * pair * width, (2 * pair + 2) * width)
+            moves[pair] = pltpu.make_async_copy(
+                result.at[:, span], out.at[:, span], done.at[pair]
+            )
+            moves[pair].start()
+    for pair in range(half):
+        moves[pair].wait()
 
 
 def whole(count):
@@ -425,11 +454,12 @@
         lambda *refs: gradient_kernel(*refs, scale=scale),
         out_shape=jax.ShapeDtypeStruct((rows, grid), F32),
         in_specs=whole(6),
-        out_specs=place,
+        out_specs=pl.BlockSpec(memory_space=pltpu.HBM),
         scratch_shapes=[
             pltpu.VMEM((4 * slabs, width), F32),
             pltpu.VMEM((width, 4 * width), F32),
             pltpu.VMEM((rows, grid), F32),
+            pltpu.SemaphoreType.DMA((grid // slabs // 2,)),
         ],
         compiler_params=limit,
         name="gradient",

time: 66.1 us -> 66.1 us (level)
  no operation moved by 1% of the time
where the time goes in v5:
time: 66.1 us; the launch traced here: 65.8 us
  blocking collectives  52 us (79%)
  Pallas kernels  5.37 us (8%)
  waiting for transfers between devices  3.99 us (6%)
  starting transfers between devices  3.48 us (5%)
  local copies, waits for them, and re-layouts  0.76 us (1%)
    all_to_all x2, blocking collectives, exchange(): lax.all_to_all(block.reshape(slabs, 4, width), 'slab', split_axis=0, conc...  52 us
    ppermute x1, waiting for transfers between devices, local(): before = lax.ppermute(tail, 'slab', ring)  3.99 us
    ppermute x1, starting transfers between devices, local(): before = lax.ppermute(tail, 'slab', ring)  3.48 us
    pallas_call x1, Pallas kernels, local(): pl.pallas_call(payload_kernel, out_shape=[jax.ShapeDtypeStruct((slabs, wi...  1.36 us
    pallas_call x1, Pallas kernels, local(): pl.pallas_call(lambda *refs: visibility_kernel(*refs, slots=slots, scale=...  1.34 us
  transfers between devices with their start and end apart: 1, of which 1 were waited for; matrix products, arithmetic and copies ran while one was open for 0% of the time, Pallas kernels for 2%

profile of v5, /device:TPU:8, one launch (start us, length us, event | category | flops | bytes accessed | tf_op | source)
XLA Modules:
  0.0 65.8 jit_solution(3061539592921832388)
XLA Ops:
  0.0 0.9 %tail.1 = bf16[8,2048]{1,0:T(8,128)(2,1)S(1)} custom-call(f32[16,2048]{1,0:T(8,128)} %image.3, f32[16,2048]{1,0:T(8,128)} %bitcast.22), custom_call_target="tpu_custom_call" | custom-call | tf_op jit(solution)/shard_map/tail/pallas_call | solution.py:387
  0.9 3.5 %collective-permute-start = (bf16[8,2048]{1,0:T(8,128)(2,1)S(1)}, bf16[8,2048]{1,0:T(8,128)(2,1)S(1)}, u32[]{:S(2)}, u32[]{:S(2)}) collective-permute-start(bf16[8,2048]{1,0:T(8,128)(2,1)S(1)} %tail.1), channel_id=1, source_target_pairs={{0,2},{2,4},{4,6},{6,8},{8,10},{10,12},{12,14},{14,16},{16,18},{18... | collective-permute-start | bytes 98312 | tf_op jit(solution)/shard_map/ppermute | solution.py:396
  4.4 0.0 copy-start.14
  4.4 0.0 copy-start.10
  4.4 0.0 copy-start.11
  4.4 0.0 copy-start.12
  4.4 0.0 copy-start.13
  4.4 0.0 copy-start.9
  4.4 0.6 copy-done.14
  5.0 0.0 copy-done.10
  5.0 0.0 copy-done.11
  5.1 0.0 copy-done.12
  5.1 0.0 copy-done.13
  5.1 0.0 copy-done.9
  5.1 1.4 %payload.1 = (f32[128,128]{1,0:T(8,128)S(1)}, f32[16,2048]{1,0:T(8,128)S(1)}, f32[16,2048]{1,0:T(8,128)S(1)}, f32[16,2048]{1,0:T(8,128)S(1)}, f32[16,2048]{1,0:T(8,128)S(1)}) custom-call(f32[16,2048]{1,0:T(8,128)} %image.3, f32[16,2048]{1,0:T(8,128)} %bitcast.23, s32[1,256]{1,0:T(1,128)S(1)} %bitcast.16, s32[1,256]{1,0:T(1,128)S(1)} %bitcast.17, ...), custom_call_target="tpu_custom_call" | custom-call | flops 30000000 | bytes 200000 | tf_op jit(solution)/shard_map/payload/pallas_call | solution.py:400
  6.5 4.0 %collective-permute-done.before = bf16[8,2048]{1,0:T(8,128)(2,1)S(1)} collective-permute-done((bf16[8,2048]{1,0:T(8,128)(2,1)S(1)}, bf16[8,2048]{1,0:T(8,128)(2,1)S(1)}, u32[]{:S(2)}, u32[]{:S(2)}) %collective-permute-start) | collective-permute-done | bytes 32800 | tf_op jit(solution)/shard_map/ppermute | solution.py:396
  10.5 0.0 copy-done
  10.5 0.0 copy-done.7
  10.5 0.0 copy-done.8
  10.5 0.0 copy-start.3
  10.5 0.0 copy-start.4
  10.5 0.0 copy-start.5
  10.5 0.0 copy-start.6
  10.5 0.5 spectrum.1
  11.1 0.0 copy-start.1
  11.1 0.0 copy-start.2
  11.1 31.6 %all_to_all.10 = bf16[128,4,128]{2,1,0:T(4,128)(2,1)S(1)} all-to-all(bf16[128,4,128]{2,1,0:T(4,128)(2,1)S(1)} %bitcast.15), channel_id=1, replica_groups=mesh['chain'=2,'slab'=128,'vis'=2] {'slab'}, dimensions={0} | all-to-all | bytes 262144 | tf_op jit(solution)/shard_map/all_to_all | solution.py:435
  42.7 0.0 copy-done.3
  42.7 0.0 copy-done.4
  42.8 1.3 %visibility.1 = bf16[512,128]{1,0:T(8,128)(2,1)S(1)} custom-call(bf16[512,128]{1,0:T(8,128)(2,1)S(1)} %bitcast.13, bf16[256,256]{1,0:T(8,128)(2,1)S(1)} %copy-done.4, bf16[256,256]{1,0:T(8,128)(2,1)S(1)} %copy-done.3, bf16[256,256]{1,0:T(8,128)(2,1)S(1)} %copy-done.2, bf16[256,256]{1,0:T(8,128)(2,1)S(1)} %copy-done.1, f32[128,128]{1,0:T(8,128)S(1)} %copy-done.6, ...), custom_call_target="tpu_custom_call" | custom-call | tf_op jit(solution)/shard_map/visibility/pallas_call | solution.py:440
  44.1 20.4 %all_to_all.11 = bf16[128,4,128]{2,1,0:T(4,128)(2,1)S(1)} all-to-all(bf16[128,4,128]{2,1,0:T(4,128)(2,1)S(1)} %bitcast.14), channel_id=1, replica_groups=mesh['chain'=2,'slab'=128,'vis'=2] {'slab'}, dimensions={0} | all-to-all | bytes 262144 | tf_op jit(solution)/shard_map/all_to_all | solution.py:435
  64.5 1.3 %gradient.1 = f32[16,2048]{1,0:T(8,128)} custom-call(bf16[512,128]{1,0:T(8,128)(2,1)S(1)} %bitcast.12, f32[16,2048]{1,0:T(8,128)S(1)} %get-tuple-element.17.refs_1_, f32[16,2048]{1,0:T(8,128)S(1)} %get-tuple-element.18.refs_2_, bf16[128,256]{1,0:T(8,128)(2,1)S(1)} %copy-done, f32[16,128]{1,0:T(8,128)S(1)} %copy-done.8, f32[16,128]{1,0:T(8,128)S(1)} %copy-done.7), custom_call_target="tpu_custom_call" | custom-call | tf_op jit(solution)/shard_map/gradient/pallas_call | solution.py:453
  (7 shorter events, 0.0 us)
Async XLA Ops:
  0.9 9.6 %collective-permute-start = (bf16[8,2048]{1,0:T(8,128)(2,1)S(1)}, bf16[8,2048]{1,0:T(8,128)(2,1)S(1)}, u32[]{:S(2)}, u32[]{:S(2)}) collective-permute-start(bf16[8,2048]{1,0:T(8,128)(2,1)S(1)} %tail.1), channel_id=1, source_target_pairs={{0,2},{2,4},{4,6},{6,8},{8,10},{10,12},{12,14},{14,16},{16,18},{18... | collective-permute-start | bytes 98312 | tf_op jit(solution)/shard_map/ppermute | solution.py:396
  4.4 0.7 %copy-start.14 = (f32[256]{0:T(256)S(1)}, f32[256]{0:T(256)}, u32[]{:S(2)}) copy-start(f32[256]{0:T(256)} %param.25) | copy-start | bytes 3076
  4.4 0.7 %copy-start.10 = (s32[256,1]{0,1:T(1,128)S(1)}, s32[256,1]{0,1:T(1,128)}, u32[]{:S(2)}) copy-start(s32[256,1]{0,1:T(1,128)} %param.21) | copy-start | bytes 3076
  4.4 0.7 %copy-start.11 = (s32[256]{0:T(256)S(1)}, s32[256]{0:T(256)}, u32[]{:S(2)}) copy-start(s32[256]{0:T(256)} %param.22) | copy-start | bytes 3076
  4.4 0.7 %copy-start.12 = (f32[256]{0:T(256)S(1)}, f32[256]{0:T(256)}, u32[]{:S(2)}) copy-start(f32[256]{0:T(256)} %param.23) | copy-start | bytes 3076
  4.4 0.7 %copy-start.13 = (f32[256]{0:T(256)S(1)}, f32[256]{0:T(256)}, u32[]{:S(2)}) copy-start(f32[256]{0:T(256)} %param.24) | copy-start | bytes 3076
  4.4 0.7 %copy-start.9 = (s32[256]{0:T(256)S(1)}, s32[256]{0:T(256)}, u32[]{:S(2)}) copy-start(s32[256]{0:T(256)} %param.20) | copy-start | bytes 3076
  5.1 5.4 %copy-start = (bf16[128,256]{1,0:T(8,128)(2,1)S(1)}, bf16[128,256]{1,0:T(8,128)(2,1)}, u32[]{:S(2)}) copy-start(bf16[128,256]{1,0:T(8,128)(2,1)} %constant.18.clone.table.refs_3_) | copy-start | bytes 196612
  5.1 5.4 %copy-start.7 = (f32[16,128]{1,0:T(8,128)S(1)}, f32[16,128]{1,0:T(8,128)}, u32[]{:S(2)}) copy-start(f32[16,128]{1,0:T(8,128)} %constant.24.clone.turn_sin.refs_5_) | copy-start | bytes 24580
  5.1 5.4 %copy-start.8 = (f32[16,128]{1,0:T(8,128)S(1)}, f32[16,128]{1,0:T(8,128)}, u32[]{:S(2)}) copy-start(f32[16,128]{1,0:T(8,128)} %constant.23.clone.turn_cos.refs_4_) | copy-start | bytes 24580
  10.5 32.2 %copy-start.3 = (bf16[256,256]{1,0:T(8,128)(2,1)S(1)}, bf16[256,256]{1,0:T(8,128)(2,1)}, u32[]{:S(2)}) copy-start(bf16[256,256]{1,0:T(8,128)(2,1)} %constant.20.clone.refs_2_) | copy-start | bytes 393220
  10.5 32.2 %copy-start.4 = (bf16[256,256]{1,0:T(8,128)(2,1)S(1)}, bf16[256,256]{1,0:T(8,128)(2,1)}, u32[]{:S(2)}) copy-start(bf16[256,256]{1,0:T(8,128)(2,1)} %constant.19.clone.refs_1_) | copy-start | bytes 393220
  10.5 32.2 %copy-start.5 = (f32[128,128]{1,0:T(8,128)S(1)}, f32[128,128]{1,0:T(8,128)}, u32[]{:S(2)}) copy-start(f32[128,128]{1,0:T(8,128)} %constant.26.clone.refs_6_) | copy-start | bytes 196612
  10.5 32.2 %copy-start.6 = (f32[128,128]{1,0:T(8,128)S(1)}, f32[128,128]{1,0:T(8,128)}, u32[]{:S(2)}) copy-start(f32[128,128]{1,0:T(8,128)} %constant.25.clone.refs_5_) | copy-start | bytes 196612
  11.1 31.7 %copy-start.1 = (bf16[256,256]{1,0:T(8,128)(2,1)S(1)}, bf16[256,256]{1,0:T(8,128)(2,1)}, u32[]{:S(2)}) copy-start(bf16[256,256]{1,0:T(8,128)(2,1)} %constant.22.clone.refs_4_) | copy-start | bytes 393220
  11.1 31.7 %copy-start.2 = (bf16[256,256]{1,0:T(8,128)(2,1)S(1)}, bf16[256,256]{1,0:T(8,128)(2,1)}, u32[]{:S(2)}) copy-start(bf16[256,256]{1,0:T(8,128)(2,1)} %constant.21.clone.refs_3_) | copy-start | bytes 393220

commit v6 on v4

--- a/solution.py
+++ b/solution.py
@@ -37,7 +37,7 @@
     cos, sin = np.kron(eye, cos), np.kron(eye, sin)
     inner = np.block([[cos, -sin], [sin, cos]])
     row_turn = [np.tile(part, (1, owned)) for part in angle(c2, shifted, grid)]
-    low = [row_forward, row_back, coarse, coarse.T, inner, inner.T]
+    low = [row_forward, row_back, coarse, coarse.T, inner.T]
     high = [*col_turn, *row_turn]
     return [jnp.asarray(t, BF16) for t in low], [jnp.asarray(t, F32) for t in high]
 
@@ -210,7 +210,7 @@
 
 
 def visibility_kernel(
-    arrived, coarse, coarse_back, inner, inner_back, turn_cos, turn_sin,
+    arrived, coarse, coarse_back, inner_back, turn_cos, turn_sin,
     out, wide, hot, spread, *, slots, scale,
 ):
     width = arrived.shape[1]
@@ -224,8 +224,8 @@
     cos, sin = turn_cos[...], turn_sin[...]
     left, right = mixed[:width], mixed[width:]
     turned = jnp.concatenate([left * cos + right * sin, right * cos - left * sin], 1)
-    cells = scale * jnp.transpose(
-        lax.dot_general(turned.astype(BF16), inner[...], NN, preferred_element_type=F32)
+    cells = scale * lax.dot_general(
+        inner_back[...], turned.astype(BF16), NT, preferred_element_type=F32
     )
     main = cells.astype(BF16)
     rest = (cells - main.astype(F32)).astype(BF16)
@@ -296,7 +296,7 @@
             grouped[down, (2 + side) * width : (3 + side) * width] = (
                 both if part == 0 else lane_roll(both, -8)
             )
-    flat = jnp.transpose(grouped[...]).astype(BF16)
+    flat = jnp.transpose(grouped[...].astype(BF16))
     mixed = lax.dot_general(flat, table[...], NN, preferred_element_type=F32)
     below = fine * rows
     real, imag = [], []
@@ -344,7 +344,7 @@
     slots = 3 * vis_row.shape[0] // slabs
     screen = screens.reshape(rows, grid)
     low, high = tables(rows, slabs, owned, grid)
-    row_forward, row_back, coarse, coarse_back, inner, inner_back = low
+    row_forward, row_back, coarse, coarse_back, inner_back = low
     col_cos, col_sin, row_cos, row_sin = high
     width = slabs
 
@@ -411,7 +411,7 @@
     back = pl.pallas_call(
         lambda *refs: visibility_kernel(*refs, slots=slots, scale=scale),
         out_shape=jax.ShapeDtypeStruct((4 * slabs, width), BF16),
-        in_specs=whole(7),
+        in_specs=whole(6),
         out_specs=place,
         scratch_shapes=[
             pltpu.VMEM((4 * slabs, width), F32),
@@ -420,7 +420,7 @@
         ],
         compiler_params=limit,
         name="visibility",
-    )(exchange(send), coarse, coarse_back, inner, inner_back, row_cos, row_sin)
+    )(exchange(send), coarse, coarse_back, inner_back, row_cos, row_sin)
     grad = pl.pallas_call(
         lambda *refs: gradient_kernel(*refs, scale=scale),
         out_shape=jax.ShapeDtypeStruct((rows, grid), F32),

time: 66.1 us -> 66 us (level)
  no operation moved by 1% of the time
where the time goes in v6:
time: 66 us; the launch traced here: 65.7 us
  blocking collectives  52 us (79%)
  Pallas kernels  5.28 us (8%)
  waiting for transfers between devices  3.99 us (6%)
  starting transfers between devices  3.48 us (5%)
  local copies, waits for them, and re-layouts  0.76 us (1%)
    all_to_all x2, blocking collectives, exchange(): lax.all_to_all(block.reshape(slabs, 4, width), 'slab', split_axis=0, conc...  52 us
    ppermute x1, waiting for transfers between devices, local(): before = lax.ppermute(tail, 'slab', ring)  3.99 us
    ppermute x1, starting transfers between devices, local(): before = lax.ppermute(tail, 'slab', ring)  3.48 us
    pallas_call x1, Pallas kernels, local(): pl.pallas_call(payload_kernel, out_shape=[jax.ShapeDtypeStruct((slabs, wi...  1.36 us
  transfers between devices with their start and end apart: 1, of which 1 were waited for; matrix products, arithmetic and copies ran while one was open for 0% of the time, Pallas kernels for 2%

profile of v6, /device:TPU:8, one launch (start us, length us, event | category | flops | bytes accessed | tf_op | source)
XLA Modules:
  0.0 65.7 jit_solution(17438200952806212796)
XLA Ops:
  0.0 0.9 %tail.1 = bf16[8,2048]{1,0:T(8,128)(2,1)S(1)} custom-call(f32[16,2048]{1,0:T(8,128)} %image.3, f32[16,2048]{1,0:T(8,128)} %bitcast.22), custom_call_target="tpu_custom_call" | custom-call | tf_op jit(solution)/shard_map/tail/pallas_call | solution.py:358
  0.9 3.5 %collective-permute-start = (bf16[8,2048]{1,0:T(8,128)(2,1)S(1)}, bf16[8,2048]{1,0:T(8,128)(2,1)S(1)}, u32[]{:S(2)}, u32[]{:S(2)}) collective-permute-start(bf16[8,2048]{1,0:T(8,128)(2,1)S(1)} %tail.1), channel_id=1, source_target_pairs={{0,2},{2,4},{4,6},{6,8},{8,10},{10,12},{12,14},{14,16},{16,18},{18... | collective-permute-start | bytes 98312 | tf_op jit(solution)/shard_map/ppermute | solution.py:367
  4.4 0.0 copy-start.13
  4.4 0.0 copy-start.9
  4.4 0.0 copy-start.10
  4.4 0.0 copy-start.11
  4.4 0.0 copy-start.12
  4.4 0.0 copy-start.8
  4.4 0.6 copy-done.13
  5.0 0.0 copy-done.9
  5.0 0.0 copy-done.10
  5.1 0.0 copy-done.11
  5.1 0.0 copy-done.12
  5.1 0.0 copy-done.8
  5.1 1.4 %payload.1 = (f32[128,128]{1,0:T(8,128)S(1)}, f32[16,2048]{1,0:T(8,128)S(1)}, f32[16,2048]{1,0:T(8,128)S(1)}, f32[16,2048]{1,0:T(8,128)S(1)}, f32[16,2048]{1,0:T(8,128)S(1)}) custom-call(f32[16,2048]{1,0:T(8,128)} %image.3, f32[16,2048]{1,0:T(8,128)} %bitcast.23, s32[1,256]{1,0:T(1,128)S(1)} %bitcast.16, s32[1,256]{1,0:T(1,128)S(1)} %bitcast.17, ...), custom_call_target="tpu_custom_call" | custom-call | flops 30000000 | bytes 200000 | tf_op jit(solution)/shard_map/payload/pallas_call | solution.py:371
  6.5 4.0 %collective-permute-done.before = bf16[8,2048]{1,0:T(8,128)(2,1)S(1)} collective-permute-done((bf16[8,2048]{1,0:T(8,128)(2,1)S(1)}, bf16[8,2048]{1,0:T(8,128)(2,1)S(1)}, u32[]{:S(2)}, u32[]{:S(2)}) %collective-permute-start) | collective-permute-done | bytes 32800 | tf_op jit(solution)/shard_map/ppermute | solution.py:367
  10.5 0.0 copy-done
  10.5 0.0 copy-done.6
  10.5 0.0 copy-done.7
  10.5 0.0 copy-start.3
  10.5 0.0 copy-start.4
  10.5 0.0 copy-start.5
  10.5 0.5 spectrum.1
  11.1 0.0 copy-start.1
  11.1 0.0 copy-start.2
  11.1 31.6 %all_to_all.10 = bf16[128,4,128]{2,1,0:T(4,128)(2,1)S(1)} all-to-all(bf16[128,4,128]{2,1,0:T(4,128)(2,1)S(1)} %bitcast.15), channel_id=1, replica_groups=mesh['chain'=2,'slab'=128,'vis'=2] {'slab'}, dimensions={0} | all-to-all | bytes 262144 | tf_op jit(solution)/shard_map/all_to_all | solution.py:406
  42.7 0.0 copy-done.3
  42.7 0.0 copy-done.4
  42.7 0.0 copy-done.5
  42.7 1.3 %visibility.1 = bf16[512,128]{1,0:T(8,128)(2,1)S(1)} custom-call(bf16[512,128]{1,0:T(8,128)(2,1)S(1)} %bitcast.13, bf16[256,256]{1,0:T(8,128)(2,1)S(1)} %copy-done.3, bf16[256,256]{1,0:T(8,128)(2,1)S(1)} %copy-done.2, bf16[256,256]{1,0:T(8,128)(2,1)S(1)} %copy-done.1, f32[128,128]{1,0:T(8,128)S(1)} %copy-done.5, f32[128,128]{1,0:T(8,128)S(1)} %copy-done.4), custom_call_target="tpu_custom_call" | custom-call | tf_op jit(solution)/shard_map/visibility/pallas_call | solution.py:411
  44.1 20.4 %all_to_all.11 = bf16[128,4,128]{2,1,0:T(4,128)(2,1)S(1)} all-to-all(bf16[128,4,128]{2,1,0:T(4,128)(2,1)S(1)} %bitcast.14), channel_id=1, replica_groups=mesh['chain'=2,'slab'=128,'vis'=2] {'slab'}, dimensions={0} | all-to-all | bytes 262144 | tf_op jit(solution)/shard_map/all_to_all | solution.py:406
  64.5 1.2 %gradient.1 = f32[16,2048]{1,0:T(8,128)} custom-call(bf16[512,128]{1,0:T(8,128)(2,1)S(1)} %bitcast.12, f32[16,2048]{1,0:T(8,128)S(1)} %get-tuple-element.17.refs_1_, f32[16,2048]{1,0:T(8,128)S(1)} %get-tuple-element.18.refs_2_, bf16[128,256]{1,0:T(8,128)(2,1)S(1)} %copy-done, f32[16,128]{1,0:T(8,128)S(1)} %copy-done.7, f32[16,128]{1,0:T(8,128)S(1)} %copy-done.6), custom_call_target="tpu_custom_call" | custom-call | tf_op jit(solution)/shard_map/gradient/pallas_call | solution.py:424
  (5 shorter events, 0.0 us)
Async XLA Ops:
  0.9 9.6 %collective-permute-start = (bf16[8,2048]{1,0:T(8,128)(2,1)S(1)}, bf16[8,2048]{1,0:T(8,128)(2,1)S(1)}, u32[]{:S(2)}, u32[]{:S(2)}) collective-permute-start(bf16[8,2048]{1,0:T(8,128)(2,1)S(1)} %tail.1), channel_id=1, source_target_pairs={{0,2},{2,4},{4,6},{6,8},{8,10},{10,12},{12,14},{14,16},{16,18},{18... | collective-permute-start | bytes 98312 | tf_op jit(solution)/shard_map/ppermute | solution.py:367
  4.4 0.7 %copy-start.13 = (f32[256]{0:T(256)S(1)}, f32[256]{0:T(256)}, u32[]{:S(2)}) copy-start(f32[256]{0:T(256)} %param.24) | copy-start | bytes 3076
  4.4 0.7 %copy-start.9 = (s32[256,1]{0,1:T(1,128)S(1)}, s32[256,1]{0,1:T(1,128)}, u32[]{:S(2)}) copy-start(s32[256,1]{0,1:T(1,128)} %param.20) | copy-start | bytes 3076
  4.4 0.7 %copy-start.10 = (s32[256]{0:T(256)S(1)}, s32[256]{0:T(256)}, u32[]{:S(2)}) copy-start(s32[256]{0:T(256)} %param.21) | copy-start | bytes 3076
  4.4 0.7 %copy-start.11 = (f32[256]{0:T(256)S(1)}, f32[256]{0:T(256)}, u32[]{:S(2)}) copy-start(f32[256]{0:T(256)} %param.22) | copy-start | bytes 3076
  4.4 0.7 %copy-start.12 = (f32[256]{0:T(256)S(1)}, f32[256]{0:T(256)}, u32[]{:S(2)}) copy-start(f32[256]{0:T(256)} %param.23) | copy-start | bytes 3076
  4.4 0.7 %copy-start.8 = (s32[256]{0:T(256)S(1)}, s32[256]{0:T(256)}, u32[]{:S(2)}) copy-start(s32[256]{0:T(256)} %param.19) | copy-start | bytes 3076
  5.1 5.4 %copy-start = (bf16[128,256]{1,0:T(8,128)(2,1)S(1)}, bf16[128,256]{1,0:T(8,128)(2,1)}, u32[]{:S(2)}) copy-start(bf16[128,256]{1,0:T(8,128)(2,1)} %constant.16.clone.table.refs_3_) | copy-start | bytes 196612
  5.1 5.4 %copy-start.6 = (f32[16,128]{1,0:T(8,128)S(1)}, f32[16,128]{1,0:T(8,128)}, u32[]{:S(2)}) copy-start(f32[16,128]{1,0:T(8,128)} %constant.21.clone.turn_sin.refs_5_) | copy-start | bytes 24580
  5.1 5.4 %copy-start.7 = (f32[16,128]{1,0:T(8,128)S(1)}, f32[16,128]{1,0:T(8,128)}, u32[]{:S(2)}) copy-start(f32[16,128]{1,0:T(8,128)} %constant.20.clone.turn_cos.refs_4_) | copy-start | bytes 24580
  10.5 32.2 %copy-start.3 = (bf16[256,256]{1,0:T(8,128)(2,1)S(1)}, bf16[256,256]{1,0:T(8,128)(2,1)}, u32[]{:S(2)}) copy-start(bf16[256,256]{1,0:T(8,128)(2,1)} %constant.17.clone.refs_1_) | copy-start | bytes 393220
  10.5 32.2 %copy-start.4 = (f32[128,128]{1,0:T(8,128)S(1)}, f32[128,128]{1,0:T(8,128)}, u32[]{:S(2)}) copy-start(f32[128,128]{1,0:T(8,128)} %constant.23.clone.refs_5_) | copy-start | bytes 196612
  10.5 32.2 %copy-start.5 = (f32[128,128]{1,0:T(8,128)S(1)}, f32[128,128]{1,0:T(8,128)}, u32[]{:S(2)}) copy-start(f32[128,128]{1,0:T(8,128)} %constant.22.clone.refs_4_) | copy-start | bytes 196612
  11.1 31.7 %copy-start.1 = (bf16[256,256]{1,0:T(8,128)(2,1)S(1)}, bf16[256,256]{1,0:T(8,128)(2,1)}, u32[]{:S(2)}) copy-start(bf16[256,256]{1,0:T(8,128)(2,1)} %constant.19.clone.refs_3_) | copy-start | bytes 393220
  11.1 31.7 %copy-start.2 = (bf16[256,256]{1,0:T(8,128)(2,1)S(1)}, bf16[256,256]{1,0:T(8,128)(2,1)}, u32[]{:S(2)}) copy-start(bf16[256,256]{1,0:T(8,128)(2,1)} %constant.18.clone.refs_2_) | copy-start | bytes 393220

commit v7 on v6

--- a/solution.py
+++ b/solution.py
@@ -205,7 +205,7 @@
                 part * deep : (part + 1) * deep, side * width : (side + 1) * width
             ]
     packed[pl.ds(2, width, stride=4), :] = pay[...]
-    packed[pl.ds(3, width, stride=4), :] = jnp.transpose(relayed[...])
+    packed[pl.ds(3, width, stride=4), :] = jnp.transpose(relayed[...].astype(BF16)).astype(F32)
     out[...] = packed[...].astype(BF16)
 
 
@@ -217,7 +217,7 @@
     wide[...] = arrived[...].astype(F32)
     part_real = wide[pl.ds(0, width, stride=4), :]
     part_imag = wide[pl.ds(1, width, stride=4), :]
-    pay = jnp.transpose(wide[pl.ds(2, width, stride=4), :])
+    pay = jnp.transpose(wide[pl.ds(2, width, stride=4), :].astype(BF16)).astype(F32)
     relayed = wide[pl.ds(3, width, stride=4), :]
     stacked = jnp.concatenate([part_real, part_imag], 0).astype(BF16)
     mixed = lax.dot_general(coarse[...], stacked, NN, preferred_element_type=F32)
@@ -285,7 +285,7 @@
     deep = width // 2
     half = fine // 2
     wide[...] = arrived[...].astype(F32)
-    next_y = jnp.transpose(wide[pl.ds(3, width, stride=4), :])
+    next_y = jnp.transpose(wide[pl.ds(3, width, stride=4), :].astype(BF16)).astype(F32)
     for side in range(2):
         both = wide[pl.ds(side * 4 + 2, deep, stride=8), :]
         for part in range(2):

time: 66 us -> 66 us (level)
  no operation moved by 1% of the time
where the time goes in v7:
time: 66 us; the launch traced here: 65.7 us
  blocking collectives  52 us (79%)
  Pallas kernels  5.27 us (8%)
  waiting for transfers between devices  3.99 us (6%)
  starting transfers between devices  3.48 us (5%)
  local copies, waits for them, and re-layouts  0.76 us (1%)
    all_to_all x2, blocking collectives, exchange(): lax.all_to_all(block.reshape(slabs, 4, width), 'slab', split_axis=0, conc...  52 us
    ppermute x1, waiting for transfers between devices, local(): before = lax.ppermute(tail, 'slab', ring)  3.99 us
    ppermute x1, starting transfers between devices, local(): before = lax.ppermute(tail, 'slab', ring)  3.48 us
    pallas_call x1, Pallas kernels, local(): pl.pallas_call(payload_kernel, out_shape=[jax.ShapeDtypeStruct((slabs, wi...  1.36 us
  transfers between devices with their start and end apart: 1, of which 1 were waited for; matrix products, arithmetic and copies ran while one was open for 0% of the time, Pallas kernels for 2%

profile of v7, /device:TPU:8, one launch (start us, length us, event | category | flops | bytes accessed | tf_op | source)
XLA Modules:
  0.0 65.7 jit_solution(5104341717527650509)
XLA Ops:
  0.0 0.9 %tail.1 = bf16[8,2048]{1,0:T(8,128)(2,1)S(1)} custom-call(f32[16,2048]{1,0:T(8,128)} %image.3, f32[16,2048]{1,0:T(8,128)} %bitcast.22), custom_call_target="tpu_custom_call" | custom-call | tf_op jit(solution)/shard_map/tail/pallas_call | solution.py:358
  0.9 3.5 %collective-permute-start = (bf16[8,2048]{1,0:T(8,128)(2,1)S(1)}, bf16[8,2048]{1,0:T(8,128)(2,1)S(1)}, u32[]{:S(2)}, u32[]{:S(2)}) collective-permute-start(bf16[8,2048]{1,0:T(8,128)(2,1)S(1)} %tail.1), channel_id=1, source_target_pairs={{0,2},{2,4},{4,6},{6,8},{8,10},{10,12},{12,14},{14,16},{16,18},{18... | collective-permute-start | bytes 98312 | tf_op jit(solution)/shard_map/ppermute | solution.py:367
  4.4 0.0 copy-start.13
  4.4 0.0 copy-start.9
  4.4 0.0 copy-start.10
  4.4 0.0 copy-start.11
  4.4 0.0 copy-start.12
  4.4 0.0 copy-start.8
  4.4 0.6 copy-done.13
  5.0 0.0 copy-done.9
  5.0 0.0 copy-done.10
  5.1 0.0 copy-done.11
  5.1 0.0 copy-done.12
  5.1 0.0 copy-done.8
  5.1 1.4 %payload.1 = (f32[128,128]{1,0:T(8,128)S(1)}, f32[16,2048]{1,0:T(8,128)S(1)}, f32[16,2048]{1,0:T(8,128)S(1)}, f32[16,2048]{1,0:T(8,128)S(1)}, f32[16,2048]{1,0:T(8,128)S(1)}) custom-call(f32[16,2048]{1,0:T(8,128)} %image.3, f32[16,2048]{1,0:T(8,128)} %bitcast.23, s32[1,256]{1,0:T(1,128)S(1)} %bitcast.16, s32[1,256]{1,0:T(1,128)S(1)} %bitcast.17, ...), custom_call_target="tpu_custom_call" | custom-call | flops 30000000 | bytes 200000 | tf_op jit(solution)/shard_map/payload/pallas_call | solution.py:371
  6.5 4.0 %collective-permute-done.before = bf16[8,2048]{1,0:T(8,128)(2,1)S(1)} collective-permute-done((bf16[8,2048]{1,0:T(8,128)(2,1)S(1)}, bf16[8,2048]{1,0:T(8,128)(2,1)S(1)}, u32[]{:S(2)}, u32[]{:S(2)}) %collective-permute-start) | collective-permute-done | bytes 32800 | tf_op jit(solution)/shard_map/ppermute | solution.py:367
  10.5 0.0 copy-done
  10.5 0.0 copy-done.6
  10.5 0.0 copy-done.7
  10.5 0.0 copy-start.3
  10.5 0.0 copy-start.4
  10.5 0.0 copy-start.5
  10.5 0.5 spectrum.1
  11.0 0.0 copy-start.1
  11.1 0.0 copy-start.2
  11.1 31.6 %all_to_all.10 = bf16[128,4,128]{2,1,0:T(4,128)(2,1)S(1)} all-to-all(bf16[128,4,128]{2,1,0:T(4,128)(2,1)S(1)} %bitcast.15), channel_id=1, replica_groups=mesh['chain'=2,'slab'=128,'vis'=2] {'slab'}, dimensions={0} | all-to-all | bytes 262144 | tf_op jit(solution)/shard_map/all_to_all | solution.py:406
  42.7 0.0 copy-done.3
  42.7 0.0 copy-done.1
  42.7 0.0 copy-done.2
  42.7 1.3 %visibility.1 = bf16[512,128]{1,0:T(8,128)(2,1)S(1)} custom-call(bf16[512,128]{1,0:T(8,128)(2,1)S(1)} %bitcast.13, bf16[256,256]{1,0:T(8,128)(2,1)S(1)} %copy-done.3, bf16[256,256]{1,0:T(8,128)(2,1)S(1)} %copy-done.2, bf16[256,256]{1,0:T(8,128)(2,1)S(1)} %copy-done.1, f32[128,128]{1,0:T(8,128)S(1)} %copy-done.5, f32[128,128]{1,0:T(8,128)S(1)} %copy-done.4), custom_call_target="tpu_custom_call" | custom-call | tf_op jit(solution)/shard_map/visibility/pallas_call | solution.py:411
  44.0 20.4 %all_to_all.11 = bf16[128,4,128]{2,1,0:T(4,128)(2,1)S(1)} all-to-all(bf16[128,4,128]{2,1,0:T(4,128)(2,1)S(1)} %bitcast.14), channel_id=1, replica_groups=mesh['chain'=2,'slab'=128,'vis'=2] {'slab'}, dimensions={0} | all-to-all | bytes 262144 | tf_op jit(solution)/shard_map/all_to_all | solution.py:406
  64.5 1.2 %gradient.1 = f32[16,2048]{1,0:T(8,128)} custom-call(bf16[512,128]{1,0:T(8,128)(2,1)S(1)} %bitcast.12, f32[16,2048]{1,0:T(8,128)S(1)} %get-tuple-element.17.refs_1_, f32[16,2048]{1,0:T(8,128)S(1)} %get-tuple-element.18.refs_2_, bf16[128,256]{1,0:T(8,128)(2,1)S(1)} %copy-done, f32[16,128]{1,0:T(8,128)S(1)} %copy-done.7, f32[16,128]{1,0:T(8,128)S(1)} %copy-done.6), custom_call_target="tpu_custom_call" | custom-call | tf_op jit(solution)/shard_map/gradient/pallas_call | solution.py:424
  (5 shorter events, 0.0 us)
Async XLA Ops:
  0.9 9.6 %collective-permute-start = (bf16[8,2048]{1,0:T(8,128)(2,1)S(1)}, bf16[8,2048]{1,0:T(8,128)(2,1)S(1)}, u32[]{:S(2)}, u32[]{:S(2)}) collective-permute-start(bf16[8,2048]{1,0:T(8,128)(2,1)S(1)} %tail.1), channel_id=1, source_target_pairs={{0,2},{2,4},{4,6},{6,8},{8,10},{10,12},{12,14},{14,16},{16,18},{18... | collective-permute-start | bytes 98312 | tf_op jit(solution)/shard_map/ppermute | solution.py:367
  4.4 0.7 %copy-start.13 = (f32[256]{0:T(256)S(1)}, f32[256]{0:T(256)}, u32[]{:S(2)}) copy-start(f32[256]{0:T(256)} %param.24) | copy-start | bytes 3076
  4.4 0.7 %copy-start.9 = (s32[256,1]{0,1:T(1,128)S(1)}, s32[256,1]{0,1:T(1,128)}, u32[]{:S(2)}) copy-start(s32[256,1]{0,1:T(1,128)} %param.20) | copy-start | bytes 3076
  4.4 0.7 %copy-start.10 = (s32[256]{0:T(256)S(1)}, s32[256]{0:T(256)}, u32[]{:S(2)}) copy-start(s32[256]{0:T(256)} %param.21) | copy-start | bytes 3076
  4.4 0.7 %copy-start.11 = (f32[256]{0:T(256)S(1)}, f32[256]{0:T(256)}, u32[]{:S(2)}) copy-start(f32[256]{0:T(256)} %param.22) | copy-start | bytes 3076
  4.4 0.7 %copy-start.12 = (f32[256]{0:T(256)S(1)}, f32[256]{0:T(256)}, u32[]{:S(2)}) copy-start(f32[256]{0:T(256)} %param.23) | copy-start | bytes 3076
  4.4 0.7 %copy-start.8 = (s32[256]{0:T(256)S(1)}, s32[256]{0:T(256)}, u32[]{:S(2)}) copy-start(s32[256]{0:T(256)} %param.19) | copy-start | bytes 3076
  5.1 5.4 %copy-start = (bf16[128,256]{1,0:T(8,128)(2,1)S(1)}, bf16[128,256]{1,0:T(8,128)(2,1)}, u32[]{:S(2)}) copy-start(bf16[128,256]{1,0:T(8,128)(2,1)} %constant.16.clone.table.refs_3_) | copy-start | bytes 196612
  5.1 5.4 %copy-start.6 = (f32[16,128]{1,0:T(8,128)S(1)}, f32[16,128]{1,0:T(8,128)}, u32[]{:S(2)}) copy-start(f32[16,128]{1,0:T(8,128)} %constant.21.clone.turn_sin.refs_5_) | copy-start | bytes 24580
  5.1 5.4 %copy-start.7 = (f32[16,128]{1,0:T(8,128)S(1)}, f32[16,128]{1,0:T(8,128)}, u32[]{:S(2)}) copy-start(f32[16,128]{1,0:T(8,128)} %constant.20.clone.turn_cos.refs_4_) | copy-start | bytes 24580
  10.5 32.2 %copy-start.3 = (bf16[256,256]{1,0:T(8,128)(2,1)S(1)}, bf16[256,256]{1,0:T(8,128)(2,1)}, u32[]{:S(2)}) copy-start(bf16[256,256]{1,0:T(8,128)(2,1)} %constant.17.clone.refs_1_) | copy-start | bytes 393220
  10.5 32.2 %copy-start.4 = (f32[128,128]{1,0:T(8,128)S(1)}, f32[128,128]{1,0:T(8,128)}, u32[]{:S(2)}) copy-start(f32[128,128]{1,0:T(8,128)} %constant.23.clone.refs_5_) | copy-start | bytes 196612
  10.5 32.2 %copy-start.5 = (f32[128,128]{1,0:T(8,128)S(1)}, f32[128,128]{1,0:T(8,128)}, u32[]{:S(2)}) copy-start(f32[128,128]{1,0:T(8,128)} %constant.22.clone.refs_4_) | copy-start | bytes 196612
  11.0 31.7 %copy-start.1 = (bf16[256,256]{1,0:T(8,128)(2,1)S(1)}, bf16[256,256]{1,0:T(8,128)(2,1)}, u32[]{:S(2)}) copy-start(bf16[256,256]{1,0:T(8,128)(2,1)} %constant.19.clone.refs_3_) | copy-start | bytes 393220
  11.1 31.7 %copy-start.2 = (bf16[256,256]{1,0:T(8,128)(2,1)S(1)}, bf16[256,256]{1,0:T(8,128)(2,1)}, u32[]{:S(2)}) copy-start(bf16[256,256]{1,0:T(8,128)(2,1)} %constant.18.clone.refs_2_) | copy-start | bytes 393220
